TPU v7x, 32 devices: a whole 2x2x4 slice. The times are simulated.
32 devices in a mesh: gx: 4 (over z), gy: 4 (over y, x), gz: 2 (over core).
Axes of the slice: x: 2, y: 2, z: 4, core: 2. Of those that a mesh axis runs over, the one named last changes fastest.
Arguments:
- features: bfloat16 [8, 16, 2, 128, 256], P('gx', 'gy', 'gz'), may hold values from -6 to 6
- fractions: bfloat16 [8, 16, 2, 3, 128], P('gx', 'gy', 'gz'), may hold values from 0 to 0.98828125
- occupied: int32 [8, 16, 2, 128], P('gx', 'gy', 'gz'), may hold values 0 or 1
- wave_index: int32 [3, 512], replicated, may hold values from -14 to 14, as said below
- radial_weight: float32 [8, 4], replicated, may hold values from -4 to 4
- ewald_mix: float32 [256, 256], replicated, may hold values from -0.375 to 0.375
- msg_weight: bfloat16 [256, 256], replicated, may hold values from -0.375 to 0.375
- ewald_weight: bfloat16 [256, 256], replicated, may hold values from -0.375 to 0.375
- out_weight: bfloat16 [256, 256], replicated, may hold values from -0.375 to 0.375
Outputs:
- updated: bfloat16 [8, 16, 2, 128, 256], P('gx', 'gy', 'gz')
Inputs may be any that keep to these rules, and one draw needn't show every extreme that they name: `wave_index`: no wavevector is zero, and no two wavevectors are equal or opposite.
All inputs are finite; a program needn't handle non-finite values. No bound on the sum of `occupied` on one device may be relied on, other than what follows from the above.
Results may differ from a plain program's by a relative error of at most 0.007.
Values may be sent and summed in bfloat16 or wider, within the bound.
A program may use at most 64 MiB of HBM per device.

v0:
```python
import functools
import math

import jax
import jax.numpy as jnp
from jax import lax
from jax.experimental import pallas as pl
from jax.experimental.pallas import tpu as pltpu
from jax.sharding import PartitionSpec as P

sharpness = 16.0
smearing = 0.04
screening = 4.0
strength = 24.0

SIN_C = [(-1.0) ** k * math.pi ** (2 * k + 1) / math.factorial(2 * k + 1) for k in range(7)]
COS_C = [(-1.0) ** k * math.pi ** (2 * k) / math.factorial(2 * k) for k in range(7)]


def poly(z, coefs):
    acc = jnp.full_like(z, coefs[-1])
    for c in coefs[-2::-1]:
        acc = acc * z + c
    return acc


def shifted(x, axis, dim, width):
    count, length = lax.axis_size(axis), x.shape[dim]
    up = [(i, (i + 1) % count) for i in range(count)]
    down = [(j, i) for i, j in up]
    last = lax.slice_in_dim(x, length - width, length, axis=dim)
    first = lax.slice_in_dim(x, 0, width, axis=dim)
    return lax.ppermute(last, axis, up), lax.ppermute(first, axis, down)


def widen(x, axis, dim):
    before, after = shifted(x, axis, dim, 1)
    return jnp.concatenate([before, x, after], axis=dim)


def message_kernel(cells_y, cells_z, fold_z, levels, home_ref, feat_ref, geom_ref, wb_ref, out_ref, hb, phi, acc):
    cell = pl.program_id(0)
    x = cell // (cells_y * cells_z)
    y = (cell // cells_z) % cells_y
    z = cell % cells_z
    slots = out_ref.shape[1]
    feat = out_ref.shape[2]
    near_z = feat_ref.shape[3]
    chunk = 32
    for a in range(3):
        hb[a] = jnp.broadcast_to(home_ref[0, :, a : a + 1], (slots, slots))
    for ox in range(3):
        for oy in range(3):
            for oz in range(near_z):
                g = geom_ref[x + ox, z, y + oy, oz]
                nx = g[0:1] + (ox - 1.0)
                ny = g[1:2] + (oy - 1.0)
                if fold_z:
                    nz = g[2:3]
                else:
                    nz = g[2:3] + (oz - 1.0)
                col = (oy * near_z + oz) * slots
                center = ox == 1 and oy == 1 and oz == (0 if fold_z else 1)
                for p0 in range(0, slots, chunk):
                    dx = nx - hb[0, p0 : p0 + chunk]
                    dy = ny - hb[1, p0 : p0 + chunk]
                    dz = nz - hb[2, p0 : p0 + chunk]
                    if fold_z and oz == 1:
                        dz = 1.0 - jnp.abs(dz)
                    radial_terms(dx, dy, dz, levels, center, p0, phi.at[ox], col, slots)
        rows = feat_ref[x + ox, z, pl.ds(y, 3)].reshape(3 * near_z * slots, feat)
        part = jnp.dot(phi[ox], rows, preferred_element_type=jnp.float32)
        if ox == 0:
            acc[...] = part
        elif ox == 1:
            acc[...] += part
    total = jnp.zeros((slots, feat), jnp.float32)
    for b in range(levels):
        both = acc[b * slots : (b + 1) * slots] + part[b * slots : (b + 1) * slots]
        total = total + both * wb_ref[b : b + 1]
    out_ref[0] = total.astype(jnp.bfloat16)


def basis_kernel(pos_ref, wave_ref, feat_ref, basis_ref, struct_ref):
    cell = pl.program_id(0)
    waves = wave_ref.shape[0]
    pos = pos_ref[0]
    chunk = 64
    for w0 in range(0, waves, chunk):
        wv = wave_ref[w0 : w0 + chunk]
        turns = wv[:, 0:1] * pos[0:1] + wv[:, 1:2] * pos[1:2] + wv[:, 2:3] * pos[2:3]
        u = turns - jnp.floor(turns + 0.5)
        q = u * u
        s = u * poly(q, SIN_C)
        c = poly(q, COS_C)
        basis_ref[0, w0 : w0 + chunk] = (1.0 - 2.0 * s * s).astype(jnp.bfloat16)
        basis_ref[0, waves + w0 : waves + w0 + chunk] = (2.0 * s * c).astype(jnp.bfloat16)
    part = jnp.dot(basis_ref[0], feat_ref[0], preferred_element_type=jnp.float32)

    @pl.when(cell == 0)
    def _():
        struct_ref[...] = part

    @pl.when(cell > 0)
    def _():
        struct_ref[...] += part


def final_kernel(basis_ref, grid_ref, msg_ref, feat_ref, home_ref, wm_ref, wo_ref, out_ref):
    far = lax.dot_general(
        basis_ref[0], grid_ref[...], (((0,), (0,)), ((), ())), preferred_element_type=jnp.float32
    )
    joined = far + jnp.dot(msg_ref[0], wm_ref[...], preferred_element_type=jnp.float32)
    hidden = (joined / (1.0 + jnp.exp(-joined))).astype(jnp.bfloat16)
    result = feat_ref[0].astype(jnp.float32) + jnp.dot(hidden, wo_ref[...], preferred_element_type=jnp.float32)
    out_ref[0] = (result * home_ref[0, :, 3:4]).astype(jnp.bfloat16)


def coords(index, counts):
    return (index // (counts[1] * counts[2]), (index // counts[2]) % counts[1], index % counts[2])


def layer_kernel(
    counts,
    levels,
    pack_ref,
    home_ref,
    pos_ref,
    wave_ref,
    wb_ref,
    damp_ref,
    mix_ref,
    we_ref,
    wm_ref,
    wo_ref,
    out_ref,
    wide,
    hb,
    phi,
    acc,
    basis,
    struct,
    pair,
    chip_sum,
    parts,
    share,
    field,
    msg,
    halo_send,
    halo_recv,
    side_send,
    side_recv,
    own_sem,
    pair_send,
    pair_recv,
    part_send,
    part_recv,
    share_send,
    share_recv,
):
    cx, cy = pack_ref.shape[0], pack_ref.shape[1]
    cells, slots, feat = out_ref.shape
    waves = wave_ref.shape[0]
    devices = counts[0] * counts[1] * counts[2]
    rows = waves // devices
    at = (lax.axis_index("gx"), lax.axis_index("gy"), lax.axis_index("gz"))
    chips = counts[0] * counts[1]
    chip = at[0] * counts[1] + at[1]
    core = at[2]
    mesh_id = pl.DeviceIdType.MESH

    partner = (at[0], at[1], 1 - core)

    def same_core(k):
        peer = (chip + k) % chips
        return (peer // counts[1], peer % counts[1], core)

    def to_partner(src, dst, send, recv):
        return pltpu.make_async_remote_copy(
            src_ref=src, dst_ref=dst, send_sem=send, recv_sem=recv, device_id=partner, device_id_type=mesh_id
        )

    barrier = pltpu.get_barrier_semaphore()

    @pl.loop(1, chips)
    def _(k):
        pl.semaphore_signal(barrier, inc=1, device_id=same_core(k), device_id_type=mesh_id)

    pl.semaphore_signal(barrier, inc=1, device_id=partner, device_id_type=mesh_id)
    pl.semaphore_wait(barrier, chips)

    own = pltpu.make_async_copy(pack_ref, wide.at[pl.ds(1, cx), pl.ds(1, cy), 0], own_sem)
    own.start()

    def span(step, length):
        if step == 0:
            return 0, 1, length
        if step == 1:
            return length - 1, 0, 1
        return 0, length + 1, 1

    halo, side = [], []
    for dx in (1, -1, 0):
        for dy in (1, -1, 0):
            n = len(halo)
            sx, tx, lx = span(dx, cx)
            sy, ty, ly = span(dy, cy)
            region = (pl.ds(tx, lx), pl.ds(ty, ly))
            if (dx, dy) == (0, 0):
                side.append(to_partner(pack_ref, wide.at[(*region, 1)], side_send.at[n], side_recv.at[n]))
                continue
            target = ((at[0] + dx + counts[0]) % counts[0], (at[1] + dy + counts[1]) % counts[1], core)
            copy = pltpu.make_async_remote_copy(
                src_ref=pack_ref.at[pl.ds(sx, lx), pl.ds(sy, ly)],
                dst_ref=wide.at[(*region, 0)],
                send_sem=halo_send.at[n],
                recv_sem=halo_recv.at[n],
                device_id=target,
                device_id_type=mesh_id,
            )
            copy.start()
            halo.append(copy)
            side.append(to_partner(wide.at[(*region, 0)], wide.at[(*region, 1)], side_send.at[n], side_recv.at[n]))
    side[-1].start()

    @pl.loop(0, cells)
    def _(cell):
        pos = pos_ref[cell]
        lanes = pl.ds(pl.multiple_of(cell * slots, slots), slots)
        chunk = 64
        for w0 in range(0, waves, chunk):
            wv = wave_ref[w0 : w0 + chunk]
            turns = wv[:, 0:1] * pos[0:1] + wv[:, 1:2] * pos[1:2] + wv[:, 2:3] * pos[2:3]
            u = turns - jnp.floor(turns + 0.5)
            q = u * u
            s = u * poly(q, SIN_C)
            c = poly(q, COS_C)
            basis[w0 : w0 + chunk, lanes] = (1.0 - 2.0 * s * s).astype(jnp.bfloat16)
            basis[waves + w0 : waves + w0 + chunk, lanes] = (2.0 * s * c).astype(jnp.bfloat16)

    atoms = pack_ref[:, :, 0:slots, :].reshape(cells * slots, feat)
    struct[...] = (
        jnp.dot(basis[...], atoms, preferred_element_type=jnp.float32)
        .astype(jnp.bfloat16)
        .reshape(2, chips, 2, rows, feat)
    )
    swap = to_partner(struct.at[:, :, 1 - core], pair, pair_send.at[0], pair_recv.at[0])
    swap.start()

    def part_copy(k):
        return pltpu.make_async_remote_copy(
            src_ref=chip_sum.at[:, (chip + k) % chips],
            dst_ref=parts.at[k],
            send_sem=part_send.at[k],
            recv_sem=part_recv.at[k],
            device_id=same_core(k),
            device_id_type=mesh_id,
        )

    def share_copy(k, slot):
        return pltpu.make_async_remote_copy(
            src_ref=share,
            dst_ref=field.at[:, slot, core],
            send_sem=share_send.at[k],
            recv_sem=share_recv.at[k],
            device_id=same_core(k),
            device_id_type=mesh_id,
        )

    def field_copy(half):
        mine = field.at[:, :, half]
        return to_partner(mine, mine, pair_send.at[1], pair_recv.at[1])

    swap.wait()
    both = struct[:, :, core].astype(jnp.float32) + pair[...].astype(jnp.float32)
    chip_sum[...] = both.astype(jnp.bfloat16)

    @pl.loop(1, chips)
    def _(k):
        part_copy(k).start()

    own.wait()
    for n, copy in enumerate(halo):
        copy.wait()
        side[n].start()
    for copy in side:
        copy.wait()

    @pl.loop(0, cells)
    def _(cell):
        @pl.when(cell == cells // 4)
        def _():
            @pl.loop(1, chips)
            def _(k):
                part_copy(k).wait()

            parts[0] = chip_sum[:, chip]
            total = jnp.sum(parts[...].astype(jnp.float32), axis=0).reshape(2 * rows, feat)
            mixed = jnp.dot(total, mix_ref[...], precision=lax.Precision.HIGHEST, preferred_element_type=jnp.float32)
            filtered = (mixed * damp_ref[...]).astype(jnp.bfloat16)
            projected = jnp.dot(filtered, we_ref[...], preferred_element_type=jnp.float32)
            projected = projected.astype(jnp.bfloat16).reshape(2, rows, feat)
            share[...] = projected
            field[:, chip, core] = projected

            @pl.loop(1, chips)
            def _(k):
                share_copy(k, chip).start()

        @pl.when(cell == cells - 1)
        def _():
            @pl.loop(1, chips)
            def _(k):
                share_copy(k, (chip - k + chips) % chips).wait()

            field_copy(core).start()

        x = cell // cy
        y = cell % cy
        for a in range(3):
            hb[a] = jnp.broadcast_to(home_ref[cell, :, a : a + 1], (slots, slots))
        chunk = 32
        for ox in range(3):
            for oy in range(3):
                for oz in range(2):
                    g = wide[x + ox, y + oy, oz, slots : slots + 16, 0:slots].astype(jnp.float32)
                    nx = g[0:1] + (ox - 1.0)
                    ny = g[1:2] + (oy - 1.0)
                    nz = g[2:3]
                    col = (oy * 2 + oz) * slots
                    for p0 in range(0, slots, chunk):
                        gx = nx - hb[0, p0 : p0 + chunk]
                        gy = ny - hb[1, p0 : p0 + chunk]
                        gz = nz - hb[2, p0 : p0 + chunk]
                        if oz == 1:
                            gz = 1.0 - jnp.abs(gz)
                        radial_terms(gx, gy, gz, levels, (ox, oy, oz) == (1, 1, 0), p0, phi.at[ox], col, slots)
            near = wide[x + ox, pl.ds(y, 3), :, 0:slots].reshape(6 * slots, feat)
            part = jnp.dot(phi[ox], near, preferred_element_type=jnp.float32)
            if ox == 0:
                acc[...] = part
            elif ox == 1:
                acc[...] += part
        total = jnp.zeros((slots, feat), jnp.float32)
        for b in range(levels):
            both = acc[b * slots : (b + 1) * slots] + part[b * slots : (b + 1) * slots]
            total = total + both * wb_ref[b : b + 1]
        msg[cell] = total.astype(jnp.bfloat16)

    field_copy(core).wait_send()
    field_copy(1 - core).wait_recv()

    waves_field = field[...].reshape(2 * waves, feat)

    @pl.loop(0, cells)
    def _(cell):
        lanes = pl.ds(pl.multiple_of(cell * slots, slots), slots)
        far = lax.dot_general(
            basis[:, lanes], waves_field, (((0,), (0,)), ((), ())), preferred_element_type=jnp.float32
        )
        joined = far + jnp.dot(msg[cell], wm_ref[...], preferred_element_type=jnp.float32)
        hidden = (joined / (1.0 + jnp.exp(-joined))).astype(jnp.bfloat16)
        atom = pack_ref[cell // cy, cell % cy, 0:slots].astype(jnp.float32)
        result = atom + jnp.dot(hidden, wo_ref[...], preferred_element_type=jnp.float32)
        out_ref[cell] = (result * home_ref[cell, :, 3:4]).astype(jnp.bfloat16)


def radial_terms(gx, gy, gz, levels, center, p0, phi, col, slots):
    rows = gx.shape[0]
    sq = jnp.minimum(gx * gx + gy * gy + gz * gz, 1.0)
    dist = sq * lax.rsqrt(jnp.maximum(sq, 1e-30))
    ratio = jnp.exp2(dist * (2.0 * sharpness / (levels - 1) * math.log2(math.e)))
    edge = 1.0 - sq
    val = edge * edge * jnp.exp2(sq * (-sharpness * math.log2(math.e)))
    if center:
        row = lax.broadcasted_iota(jnp.int32, val.shape, 0) + p0
        lane = lax.broadcasted_iota(jnp.int32, val.shape, 1)
        val = jnp.where(row == lane, 0.0, val)
    for b in range(levels):
        phi[b * slots + p0 : b * slots + p0 + rows, col : col + slots] = val.astype(jnp.bfloat16)
        if b + 1 < levels:
            val = val * ratio


def body(
    features,
    fractions,
    occupied,
    wave_index,
    radial_weight,
    ewald_mix,
    msg_weight,
    ewald_weight,
    out_weight,
):
    cx, cy, cz, slots, feat = features.shape
    levels, heads = radial_weight.shape
    cells = cx * cy * cz
    grid = [lax.axis_size("gx") * cx, lax.axis_size("gy") * cy, lax.axis_size("gz") * cz]
    devices = lax.axis_size("gx") * lax.axis_size("gy") * lax.axis_size("gz")
    waves = wave_index.shape[1]
    axes = ("gx", "gy", "gz")
    full = lambda shape: pl.BlockSpec(shape, lambda i: (0,) * len(shape))
    params = pltpu.CompilerParams(dimension_semantics=("arbitrary",), vmem_limit_bytes=56 * 2**20)

    masked = features * occupied[..., None].astype(jnp.bfloat16)
    frac = fractions.astype(jnp.float32)
    cell_feat = masked.reshape(cells, slots, feat)
    home = jnp.concatenate([frac, occupied[:, :, :, None, :].astype(jnp.float32)], axis=3)
    home = jnp.swapaxes(home.reshape(cells, 4, slots), 1, 2)

    start = [
        (lax.axis_index(n) * c + jnp.arange(c, dtype=jnp.int32)).astype(jnp.float32)
        for n, c in zip(axes, (cx, cy, cz))
    ]
    origin = jnp.stack(jnp.meshgrid(*start, indexing="ij"), axis=-1)[..., None]
    pos = (origin + frac).reshape(cells, 3, slots)
    lengths = jnp.array(grid, jnp.float32)
    index = wave_index.astype(jnp.float32)
    wave_vec = 2.0 * math.pi * index / lengths[:, None]
    wave_sq = jnp.sum(wave_vec * wave_vec, axis=0)
    damping = (
        strength
        * jnp.exp(-0.5 * smearing * wave_sq)
        / (wave_sq + screening)
        * (1.0 / math.sqrt(cells * slots * devices * waves))
    )
    wave_turn = (index / lengths[:, None]).T

    fold_z = grid[2] == 2 and cz == 1
    level = jnp.arange(levels, dtype=jnp.float32) / (levels - 1)
    wb = radial_weight * (jnp.exp(-sharpness * level * level) / math.sqrt(4.0 * slots))[:, None]
    wb = jnp.repeat(wb, feat // heads, axis=1)
    counts = tuple(lax.axis_size(n) for n in axes)
    rows = waves // devices
    chips = counts[0] * counts[1]
    if fold_z and rows % 16 == 0 and min(counts) > 1:
        spread = jnp.pad(fractions, ((0, 0),) * 3 + ((0, 13), (0, feat - slots)))
        pack = jnp.concatenate([masked, spread], axis=3).reshape(cx, cy, slots + 16, feat)
        damp = lax.dynamic_slice_in_dim(damping, lax.axis_index(axes) * rows, rows, 0)
        damp = jnp.concatenate([damp, damp]).reshape(2 * rows, 1)
        vmem = pl.BlockSpec(memory_space=pltpu.VMEM)
        dma = pltpu.SemaphoreType.DMA
        out = pl.pallas_call(
            functools.partial(layer_kernel, counts, levels),
            in_specs=[vmem] * 10,
            out_specs=vmem,
            out_shape=jax.ShapeDtypeStruct((cells, slots, feat), jnp.bfloat16),
            scratch_shapes=[
                pltpu.VMEM((cx + 2, cy + 2, 2, slots + 16, feat), jnp.bfloat16),
                pltpu.VMEM((3, slots, slots), jnp.float32),
                pltpu.VMEM((3, levels * slots, 6 * slots), jnp.bfloat16),
                pltpu.VMEM((levels * slots, feat), jnp.float32),
                pltpu.VMEM((2 * waves, cells * slots), jnp.bfloat16),
                pltpu.VMEM((2, chips, 2, rows, feat), jnp.bfloat16),
                pltpu.VMEM((2, chips, rows, feat), jnp.bfloat16),
                pltpu.VMEM((2, chips, rows, feat), jnp.bfloat16),
                pltpu.VMEM((chips, 2, rows, feat), jnp.bfloat16),
                pltpu.VMEM((2, rows, feat), jnp.bfloat16),
                pltpu.VMEM((2, chips, 2, rows, feat), jnp.bfloat16),
                pltpu.VMEM((cells, slots, feat), jnp.bfloat16),
                dma((8,)),
                dma((8,)),
                dma((9,)),
                dma((9,)),
                dma,
                dma((2,)),
                dma((2,)),
                dma((chips,)),
                dma((chips,)),
                dma((chips,)),
                dma((chips,)),
            ],
            compiler_params=pltpu.CompilerParams(
                collective_id=0, has_side_effects=True, vmem_limit_bytes=56 * 2**20
            ),
            name="layer",
        )(pack, home, pos, wave_turn, wb, damp, ewald_mix, ewald_weight, msg_weight, out_weight)
        return out.reshape(features.shape)

    basis, struct = pl.pallas_call(
        basis_kernel,
        grid=(cells,),
        in_specs=[
            pl.BlockSpec((1, 3, slots), lambda i: (i, 0, 0)),
            full((waves, 3)),
            pl.BlockSpec((1, slots, feat), lambda i: (i, 0, 0)),
        ],
        out_specs=[pl.BlockSpec((1, 2 * waves, slots), lambda i: (i, 0, 0)), full((2 * waves, feat))],
        out_shape=[
            jax.ShapeDtypeStruct((cells, 2 * waves, slots), jnp.bfloat16),
            jax.ShapeDtypeStruct((2 * waves, feat), jnp.float32),
        ],
        compiler_params=params,
        name="basis",
    )(pos, wave_turn, cell_feat)

    wave_share = lax.psum_scatter(struct.reshape(2, waves, feat), axes, scatter_dimension=1, tiled=True)
    share_rows = wave_share.shape[1]
    share_damp = lax.dynamic_slice_in_dim(damping, lax.axis_index(axes) * share_rows, share_rows, 0)
    mixed = jnp.dot(wave_share.reshape(2 * share_rows, feat), ewald_mix, precision=lax.Precision.HIGHEST)
    filtered = (mixed.reshape(2, share_rows, feat) * share_damp[None, :, None]).astype(jnp.bfloat16)
    projected = jnp.dot(filtered, ewald_weight, preferred_element_type=jnp.float32).astype(jnp.bfloat16)
    field = lax.all_gather(projected, axes, axis=1, tiled=True).reshape(2 * waves, feat)

    wide_feat = widen(widen(masked, "gx", 0), "gy", 1)
    wide_geom = widen(widen(fractions, "gx", 0), "gy", 1)
    if fold_z:
        swap = [(0, 1), (1, 0)]
        wide_feat = jnp.concatenate([wide_feat, lax.ppermute(wide_feat, "gz", swap)], axis=2)
        wide_geom = jnp.concatenate([wide_geom, lax.ppermute(wide_geom, "gz", swap)], axis=2)
        near_z = 2
    else:
        wide_feat = widen(wide_feat, "gz", 2)
        wide_geom = widen(wide_geom, "gz", 2)
        near_z = 3
    wide_feat = jnp.stack([wide_feat[:, :, z : z + near_z] for z in range(cz)], axis=1)
    wide_geom = jnp.stack([wide_geom[:, :, z : z + near_z] for z in range(cz)], axis=1).astype(jnp.float32)
    messages = pl.pallas_call(
        functools.partial(message_kernel, cy, cz, fold_z, levels),
        grid=(cells,),
        in_specs=[
            pl.BlockSpec((1, slots, 4), lambda i: (i, 0, 0)),
            full(wide_feat.shape),
            full(wide_geom.shape),
            full(wb.shape),
        ],
        out_specs=pl.BlockSpec((1, slots, feat), lambda i: (i, 0, 0)),
        out_shape=jax.ShapeDtypeStruct((cells, slots, feat), jnp.bfloat16),
        scratch_shapes=[
            pltpu.VMEM((3, slots, slots), jnp.float32),
            pltpu.VMEM((3, levels * slots, 3 * near_z * slots), jnp.bfloat16),
            pltpu.VMEM((levels * slots, feat), jnp.float32),
        ],
        compiler_params=params,
        cost_estimate=pl.CostEstimate(
            flops=2 * cells * levels * slots * 9 * near_z * slots * feat, bytes_accessed=2**22, transcendentals=0
        ),
        name="messages",
    )(home, wide_feat, wide_geom, wb)

    out = pl.pallas_call(
        final_kernel,
        grid=(cells,),
        in_specs=[
            pl.BlockSpec((1, 2 * waves, slots), lambda i: (i, 0, 0)),
            full((2 * waves, feat)),
            pl.BlockSpec((1, slots, feat), lambda i: (i, 0, 0)),
            pl.BlockSpec((1, slots, feat), lambda i: (i, 0, 0)),
            pl.BlockSpec((1, slots, 4), lambda i: (i, 0, 0)),
            full((feat, feat)),
            full((feat, feat)),
        ],
        out_specs=pl.BlockSpec((1, slots, feat), lambda i: (i, 0, 0)),
        out_shape=jax.ShapeDtypeStruct((cells, slots, feat), jnp.bfloat16),
        compiler_params=params,
        name="final",
    )(basis, field, messages, cell_feat, home, msg_weight, out_weight)
    return out.reshape(features.shape)


def solution(mesh):
    cell = P("gx", "gy", "gz", None, None)
    in_specs = (cell, cell, P("gx", "gy", "gz", None), P(), P(), P(), P(), P(), P())
    return jax.shard_map(body, mesh=mesh, in_specs=in_specs, out_specs=cell, check_vma=False)
```

profile of v0, /device:TPU:0, one launch (start us, length us, event | category | flops | bytes accessed | tf_op | source)
XLA Modules:
  0.0 64.5 jit_solution(3025217919980628582)
XLA Ops:
  0.0 0.8 %fusion.3 = (f32[512]{0:T(512)S(1)}, f32[3,512]{1,0:T(4,128)S(1)}) fusion(s32[3,512]{1,0:T(4,128)} %param.13, f32[3]{0:T(128)} %constant.54), kind=kLoop, calls=%fused_computation.7 | loop fusion | flops 8704 | bytes 14348 | tf_op jit(solution)/shard_map/reduce_sum | solution.py:421
  0.8 0.0 copy-start
  0.8 0.1 dynamic_slice.3
  0.9 0.1 maximum_bitcast_fusion.1
  1.0 0.7 %copy.61.damp_ref = f32[32,1]{1,0:T(8,128)} copy(f32[32,1]{0,1:T(1,128)S(1)} %maximum_bitcast_fusion.1) | data formatting | bytes 256 | tf_op jit(solution)/shard_map/reshape | solution.py:441
  1.7 0.1 stack_broadcast_in_dim.9
  1.7 0.1 pad.9.clone
  1.8 0.1 maximum_bitcast_fusion
  1.9 0.8 %broadcast_add_fusion = f32[2,4,1,3,128]{4,1,3,2,0:T(4,128)S(1)} fusion(f32[2,4,3]{1,2,0:T(4,128)S(1)} %copy.56, bf16[2,4,1,3,128]{4,1,3,2,0:T(4,128)(2,1)} %param.11), kind=kLoop, calls=%fused_computation.9 | loop fusion | flops 6144 | bytes 18528 | tf_op jit(solution)/shard_map/add | solution.py:417
  2.7 0.6 copy.57
  3.3 0.8 %fusion.8 = (f32[2,4,1,128]{3,2,1,0:T(1,128)S(1)}, bf16[2,4,1,128]{3,2,1,0:T(2,128)(2,1)S(1)}) fusion(s32[2,4,1,128]{3,2,1,0:T(1,128)} %param.12), kind=kLoop, calls=%fused_computation.23 | loop fusion | flops 2048 | bytes 10240 | tf_op jit(solution)/shard_map/convert_element_type | solution.py:409
  4.0 1.2 %bitcast_multiply_fusion = bf16[2,4,1,128,256]{4,3,1,0,2:T(8,128)(2,1)S(1)} fusion(bf16[2,4,1,128,256]{4,3,2,1,0:T(8,128)(2,1)} %param.10, bf16[2,4,128]{2,1,0:T(4,128)(2,1)S(1)} %bitcast.26), kind=kLoop, calls=%fused_computation.4 | loop fusion | flops 262144 | bytes 1050624 | tf_op jit(solution)/shard_map/mul | solution.py:406
  5.3 0.0 copy-done
  5.3 0.8 %fusion.2.pack_ref = bf16[2,4,144,256]{3,2,1,0:T(8,128)(2,1)} fusion(bf16[2,4,1,3,128]{4,3,1,0,2:T(4,128)(2,1)S(1)} %copy.53, bf16[2,4,1,128,256]{4,3,1,0,2:T(8,128)(2,1)S(1)} %bitcast_multiply_fusion), kind=kLoop, calls=%fused_computation.3 | loop fusion | flops 1769472 | bytes 1120256 | tf_op jit(solution)/shard_map/reshape | solution.py:439
  6.2 0.0 copy-start.1
  6.2 1.0 %copy.55 = f32[8,4,128]{1,2,0:T(8,128)} copy(f32[8,4,128]{2,0,1:T(8,128)S(1)} %pad_maximum_fusion) | data formatting | bytes 32768 | tf_op jit(solution)/shard_map/concatenate | solution.py:409
  7.2 0.8 %copy.58 = f32[3,512]{0,1:T(8,128)} copy(f32[3,512]{1,0:T(4,128)S(1)} %get-tuple-element.6) | data formatting | bytes 12288 | tf_op jit(solution)/shard_map/div | solution.py:428
  8.1 0.0 copy-done.1
  8.1 0.1 copy.59
  8.2 0.1 broadcast_in_dim.2
  8.2 0.7 %reshape.60.wb_ref = f32[8,256]{1,0:T(8,128)} reshape(f32[8,4,64]{2,1,0:T(4,128)S(1)} %broadcast_in_dim.2) | data formatting | bytes 16384 | tf_op jit(solution)/shard_map/reshape | solution.py:433
  8.9 53.7 %layer.1 = bf16[8,128,256]{2,1,0:T(8,128)(2,1)} custom-call(bf16[2,4,144,256]{3,2,1,0:T(8,128)(2,1)} %fusion.2.pack_ref, f32[8,128,4]{2,1,0:T(8,128)} %bitcast.20, f32[8,3,128]{2,1,0:T(4,128)} %bitcast.23, f32[512,3]{1,0:T(8,128)} %bitcast.22, f32[8,256]{1,0:T(8,128)} %reshape.60.wb_ref, f32[32,1]{1,0:T(8,128)} %copy.61.damp_ref, f32[256,256]{1,0:T(8,128)} %mix_ref.1, ...), custom_call_target="tpu_custom_call" | custom-call | tf_op jit(solution)/shard_map/layer/pallas_call | solution.py:444
  62.6 1.9 %copy.68 = bf16[2,4,1,128,256]{4,3,2,1,0:T(8,128)(2,1)} copy(bf16[2,4,1,128,256]{4,3,2,1,0:T(8,128)(2,1)} %bitcast.21) | data formatting | bytes 1048576
  (11 shorter events, 0.1 us)
Async XLA Ops:
  0.8 4.5 %copy-start = (bf16[2,4,1,3,128]{4,1,3,2,0:T(4,128)(2,1)S(1)}, bf16[2,4,1,3,128]{4,1,3,2,0:T(4,128)(2,1)}, u32[]{:S(2)}) copy-start(bf16[2,4,1,3,128]{4,1,3,2,0:T(4,128)(2,1)} %param.11) | copy-start | bytes 18436
  6.2 1.9 %copy-start.1 = (f32[8,4]{0,1:T(4,128)S(1)}, f32[8,4]{0,1:T(4,128)}, u32[]{:S(2)}) copy-start(f32[8,4]{0,1:T(4,128)} %param.14) | copy-start | bytes 388
where the time goes:
time: 64.8 us; the launch traced here: 64.5 us
  Pallas kernels  53.7 us (83%)
  local copies, waits for them, and re-layouts  6.14 us (9%)
  other arithmetic  4.6 us (7%)
    pallas_call x1, Pallas kernels, body(): pl.pallas_call(functools.partial(layer_kernel, counts, levels), in_specs=...  53.7 us
    unnamed x7, local copies, waits for them, and re-layouts  1.89 us

commit v1 on v0

--- a/solution.py
+++ b/solution.py
@@ -123,21 +123,24 @@
 def layer_kernel(
     counts,
     levels,
-    pack_ref,
-    home_ref,
-    pos_ref,
-    wave_ref,
-    wb_ref,
-    damp_ref,
+    feat_ref,
+    frac_ref,
+    occ_ref,
+    index_ref,
+    radial_ref,
     mix_ref,
     we_ref,
     wm_ref,
     wo_ref,
     out_ref,
     wide,
+    rows_sc,
+    out_mask,
+    turn_cols,
+    wb,
     hb,
     phi,
-    acc,
+    msg,
     basis,
     struct,
     pair,
@@ -145,12 +148,10 @@
     parts,
     share,
     field,
-    msg,
     halo_send,
     halo_recv,
     side_send,
     side_recv,
-    own_sem,
     pair_send,
     pair_recv,
     part_send,
@@ -158,16 +159,19 @@
     share_send,
     share_recv,
 ):
-    cx, cy = pack_ref.shape[0], pack_ref.shape[1]
-    cells, slots, feat = out_ref.shape
-    waves = wave_ref.shape[0]
+    cx, cy, slots, feat = feat_ref.shape
+    cells = cx * cy
+    waves = index_ref.shape[1]
+    heads = radial_ref.shape[0]
     devices = counts[0] * counts[1] * counts[2]
+    grid = (counts[0] * cx, counts[1] * cy, counts[2])
     rows = waves // devices
     at = (lax.axis_index("gx"), lax.axis_index("gy"), lax.axis_index("gz"))
     chips = counts[0] * counts[1]
     chip = at[0] * counts[1] + at[1]
     core = at[2]
     mesh_id = pl.DeviceIdType.MESH
+    pad = wide.shape[3] - slots
 
     partner = (at[0], at[1], 1 - core)
 
@@ -187,50 +191,85 @@
         pl.semaphore_signal(barrier, inc=1, device_id=same_core(k), device_id_type=mesh_id)
 
     pl.semaphore_signal(barrier, inc=1, device_id=partner, device_id_type=mesh_id)
+
+    rows_sc[...] = jnp.zeros_like(rows_sc)
+    for x in range(cx):
+        for a in range(3):
+            k = (x * 3 + a) * cy
+            rows_sc[k : k + cy] = frac_ref[x, a].astype(jnp.float32)
+    rows_sc[3 * cells : 4 * cells] = occ_ref[...].astype(jnp.float32)
+    turned = rows_sc[...].T
+    for x in range(cx):
+        for y in range(cy):
+            cell = x * cy + y
+            ks = [(x * 3 + a) * cy + y for a in range(3)]
+            there = jnp.broadcast_to(turned[:, 3 * cells + cell : 3 * cells + cell + 1], (slots, feat))
+            wide[1 + x, 1 + y, 0, 0:slots] = feat_ref[x, y] * there.astype(jnp.bfloat16)
+            own = jnp.concatenate([rows_sc[k : k + 1] for k in ks] + [jnp.zeros((pad - 3, slots), jnp.float32)])
+            own = jnp.concatenate([own, jnp.zeros((pad, feat - slots), jnp.float32)], axis=1)
+            wide[1 + x, 1 + y, 0, slots:] = own.astype(jnp.bfloat16)
+
     pl.semaphore_wait(barrier, chips)
-
-    own = pltpu.make_async_copy(pack_ref, wide.at[pl.ds(1, cx), pl.ds(1, cy), 0], own_sem)
-    own.start()
 
     def span(step, length):
         if step == 0:
-            return 0, 1, length
+            return 1, 1, length
         if step == 1:
-            return length - 1, 0, 1
-        return 0, length + 1, 1
-
-    halo, side = [], []
-    for dx in (1, -1, 0):
-        for dy in (1, -1, 0):
-            n = len(halo)
-            sx, tx, lx = span(dx, cx)
-            sy, ty, ly = span(dy, cy)
-            region = (pl.ds(tx, lx), pl.ds(ty, ly))
-            if (dx, dy) == (0, 0):
-                side.append(to_partner(pack_ref, wide.at[(*region, 1)], side_send.at[n], side_recv.at[n]))
-                continue
-            target = ((at[0] + dx + counts[0]) % counts[0], (at[1] + dy + counts[1]) % counts[1], core)
-            copy = pltpu.make_async_remote_copy(
-                src_ref=pack_ref.at[pl.ds(sx, lx), pl.ds(sy, ly)],
-                dst_ref=wide.at[(*region, 0)],
-                send_sem=halo_send.at[n],
-                recv_sem=halo_recv.at[n],
-                device_id=target,
-                device_id_type=mesh_id,
-            )
-            copy.start()
-            halo.append(copy)
-            side.append(to_partner(wide.at[(*region, 0)], wide.at[(*region, 1)], side_send.at[n], side_recv.at[n]))
-    side[-1].start()
+            return length, 0, 1
+        return 1, length + 1, 1
+
+    halo, side = {}, {}
+    for n, (dx, dy) in enumerate([(0, 1), (0, -1), (1, 0), (-1, 0), (1, 1), (1, -1), (-1, 1), (-1, -1), (0, 0)]):
+        sx, tx, lx = span(dx, cx)
+        sy, ty, ly = span(dy, cy)
+        region = (pl.ds(tx, lx), pl.ds(ty, ly))
+        side[dx, dy] = to_partner(wide.at[(*region, 0)], wide.at[(*region, 1)], side_send.at[n], side_recv.at[n])
+        if (dx, dy) == (0, 0):
+            continue
+        target = ((at[0] + dx + counts[0]) % counts[0], (at[1] + dy + counts[1]) % counts[1], core)
+        halo[dx, dy] = pltpu.make_async_remote_copy(
+            src_ref=wide.at[pl.ds(sx, lx), pl.ds(sy, ly), 0],
+            dst_ref=wide.at[(*region, 0)],
+            send_sem=halo_send.at[n],
+            recv_sem=halo_recv.at[n],
+            device_id=target,
+            device_id_type=mesh_id,
+        )
+    side[0, 0].start()
+    for copy in halo.values():
+        copy.start()
+
+    for x in range(cx):
+        for y in range(cy):
+            for a in range(3):
+                k = (x * 3 + a) * cy + y
+                hb[x * cy + y, a] = jnp.broadcast_to(turned[:, k : k + 1], (slots, slots))
+            k = 3 * cells + x * cy + y
+            out_mask[x * cy + y] = jnp.broadcast_to(turned[:, k : k + 1], (slots, feat))
+    for w0 in range(0, waves, 128):
+        part = [index_ref[a : a + 1, w0 : w0 + 128].astype(jnp.float32) * (1.0 / grid[a]) for a in range(3)]
+        part = jnp.concatenate(part + [jnp.zeros((5, 128), jnp.float32)])
+        turn_cols[w0 : w0 + 128] = part.T
+    owner = lax.broadcasted_iota(jnp.int32, (heads, feat), 1) // (feat // heads)
+    mine = owner == lax.broadcasted_iota(jnp.int32, (heads, feat), 0)
+    for b in range(levels):
+        level = b / (levels - 1)
+        scale = math.exp(-sharpness * level * level) / math.sqrt(4.0 * slots)
+        column = jnp.broadcast_to(radial_ref[:, b : b + 1], (heads, feat)) * scale
+        wb[b : b + 1] = jnp.sum(jnp.where(mine, column, 0.0), axis=0, keepdims=True)
 
     @pl.loop(0, cells)
     def _(cell):
-        pos = pos_ref[cell]
+        x = cell // cy
+        y = cell % cy
+        first = (x * 3) * cy + y
+        start = [(at[0] * cx + x).astype(jnp.float32), (at[1] * cy + y).astype(jnp.float32), core.astype(jnp.float32)]
+        pos = [rows_sc[pl.ds(first + a * cy, 1)] + start[a] for a in range(3)]
         lanes = pl.ds(pl.multiple_of(cell * slots, slots), slots)
         chunk = 64
         for w0 in range(0, waves, chunk):
-            wv = wave_ref[w0 : w0 + chunk]
-            turns = wv[:, 0:1] * pos[0:1] + wv[:, 1:2] * pos[1:2] + wv[:, 2:3] * pos[2:3]
+            wv = turn_cols[w0 : w0 + chunk]
+            turns = wv[:, 0:1] * pos[0] + wv[:, 1:2] * pos[1] + wv[:, 2:3] * pos[2]
             u = turns - jnp.floor(turns + 0.5)
             q = u * u
             s = u * poly(q, SIN_C)
@@ -238,7 +277,7 @@
             basis[w0 : w0 + chunk, lanes] = (1.0 - 2.0 * s * s).astype(jnp.bfloat16)
             basis[waves + w0 : waves + w0 + chunk, lanes] = (2.0 * s * c).astype(jnp.bfloat16)
 
-    atoms = pack_ref[:, :, 0:slots, :].reshape(cells * slots, feat)
+    atoms = wide[1 : 1 + cx, 1 : 1 + cy, 0, 0:slots].reshape(cells * slots, feat)
     struct[...] = (
         jnp.dot(basis[...], atoms, preferred_element_type=jnp.float32)
         .astype(jnp.bfloat16)
@@ -246,6 +285,7 @@
     )
     swap = to_partner(struct.at[:, :, 1 - core], pair, pair_send.at[0], pair_recv.at[0])
     swap.start()
+    msg[...] = jnp.zeros_like(msg)
 
     def part_copy(k):
         return pltpu.make_async_remote_copy(
@@ -271,81 +311,119 @@
         mine = field.at[:, :, half]
         return to_partner(mine, mine, pair_send.at[1], pair_recv.at[1])
 
-    swap.wait()
-    both = struct[:, :, core].astype(jnp.float32) + pair[...].astype(jnp.float32)
-    chip_sum[...] = both.astype(jnp.bfloat16)
-
-    @pl.loop(1, chips)
-    def _(k):
-        part_copy(k).start()
-
-    own.wait()
-    for n, copy in enumerate(halo):
-        copy.wait()
-        side[n].start()
-    for copy in side:
-        copy.wait()
-
-    @pl.loop(0, cells)
-    def _(cell):
-        @pl.when(cell == cells // 4)
-        def _():
-            @pl.loop(1, chips)
-            def _(k):
-                part_copy(k).wait()
-
-            parts[0] = chip_sum[:, chip]
-            total = jnp.sum(parts[...].astype(jnp.float32), axis=0).reshape(2 * rows, feat)
-            mixed = jnp.dot(total, mix_ref[...], precision=lax.Precision.HIGHEST, preferred_element_type=jnp.float32)
-            filtered = (mixed * damp_ref[...]).astype(jnp.bfloat16)
-            projected = jnp.dot(filtered, we_ref[...], preferred_element_type=jnp.float32)
-            projected = projected.astype(jnp.bfloat16).reshape(2, rows, feat)
-            share[...] = projected
-            field[:, chip, core] = projected
-
-            @pl.loop(1, chips)
-            def _(k):
-                share_copy(k, chip).start()
-
-        @pl.when(cell == cells - 1)
-        def _():
-            @pl.loop(1, chips)
-            def _(k):
-                share_copy(k, (chip - k + chips) % chips).wait()
-
-            field_copy(core).start()
-
-        x = cell // cy
-        y = cell % cy
-        for a in range(3):
-            hb[a] = jnp.broadcast_to(home_ref[cell, :, a : a + 1], (slots, slots))
+    def sum_pair():
+        swap.wait()
+        both = struct[:, :, core].astype(jnp.float32) + pair[...].astype(jnp.float32)
+        chip_sum[...] = both.astype(jnp.bfloat16)
+
+        @pl.loop(1, chips)
+        def _(k):
+            part_copy(k).start()
+
+    def filter_share():
+        @pl.loop(1, chips)
+        def _(k):
+            part_copy(k).wait()
+
+        parts[0] = chip_sum[:, chip]
+        total = jnp.sum(parts[...].astype(jnp.float32), axis=0).reshape(2 * rows, feat)
+        mixed = jnp.dot(total, mix_ref[...], precision=lax.Precision.HIGHEST, preferred_element_type=jnp.float32)
+        vec = turn_cols[pl.ds((chip * 2 + core) * rows, rows)] * (2.0 * math.pi)
+        square = jnp.sum(vec * vec, axis=1, keepdims=True)
+        damp = strength * jnp.exp(-0.5 * smearing * square) / (square + screening)
+        damp = damp * (1.0 / math.sqrt(cells * slots * devices * waves))
+        filtered = (mixed * jnp.concatenate([damp, damp])).astype(jnp.bfloat16)
+        projected = jnp.dot(filtered, we_ref[...], preferred_element_type=jnp.float32)
+        projected = projected.astype(jnp.bfloat16).reshape(2, rows, feat)
+        share[...] = projected
+        field[:, chip, core] = projected
+
+        @pl.loop(1, chips)
+        def _(k):
+            share_copy(k, chip).start()
+
+    def join_field():
+        @pl.loop(1, chips)
+        def _(k):
+            share_copy(k, (chip - k + chips) % chips).wait()
+
+        field_copy(core).start()
+
+    def place(x, j):
+        late = j // (2 * cy)
+        xi = (1 - late) * (1 + j % 2) + late * (x * (cx + 1))
+        y = ((1 - late) * (j // 2) + late * (j - 2 * cy) + 1) % cy
+        return xi, y
+
+    def weigh(x, j):
+        xi, y = place(x, j)
+        cell = x * cy + y
+        step = xi - (x + 1)
         chunk = 32
-        for ox in range(3):
-            for oy in range(3):
-                for oz in range(2):
-                    g = wide[x + ox, y + oy, oz, slots : slots + 16, 0:slots].astype(jnp.float32)
-                    nx = g[0:1] + (ox - 1.0)
-                    ny = g[1:2] + (oy - 1.0)
-                    nz = g[2:3]
-                    col = (oy * 2 + oz) * slots
-                    for p0 in range(0, slots, chunk):
-                        gx = nx - hb[0, p0 : p0 + chunk]
-                        gy = ny - hb[1, p0 : p0 + chunk]
-                        gz = nz - hb[2, p0 : p0 + chunk]
-                        if oz == 1:
-                            gz = 1.0 - jnp.abs(gz)
-                        radial_terms(gx, gy, gz, levels, (ox, oy, oz) == (1, 1, 0), p0, phi.at[ox], col, slots)
-            near = wide[x + ox, pl.ds(y, 3), :, 0:slots].reshape(6 * slots, feat)
-            part = jnp.dot(phi[ox], near, preferred_element_type=jnp.float32)
-            if ox == 0:
-                acc[...] = part
-            elif ox == 1:
-                acc[...] += part
-        total = jnp.zeros((slots, feat), jnp.float32)
+        for oy in range(3):
+            for oz in range(2):
+                g = wide[xi, y + oy, oz, slots : slots + pad, 0:slots].astype(jnp.float32)
+                nx = g[0:1] + step.astype(jnp.float32)
+                ny = g[1:2] + (oy - 1.0)
+                nz = g[2:3]
+                col = oy * 2 + oz
+                for p0 in range(0, slots, chunk):
+                    gx = nx - hb[cell, 0, p0 : p0 + chunk]
+                    gy = ny - hb[cell, 1, p0 : p0 + chunk]
+                    gz = nz - hb[cell, 2, p0 : p0 + chunk]
+                    if oz == 1:
+                        gz = 1.0 - jnp.abs(gz)
+                    diagonal = p0 + step * slots if (oy, oz) == (1, 0) else None
+                    radial_chain(gx, gy, gz, levels, diagonal, p0, phi.at[x, col], slots)
+
+    def gather(x, j):
+        xi, y = place(x, j)
+        cell = x * cy + y
+        near = wide[xi, pl.ds(y, 3), :, 0:slots].reshape(6 * slots, feat)
+        left = jnp.concatenate([phi[x, col] for col in range(6)], axis=1)
+        part = jnp.dot(left, near, preferred_element_type=jnp.float32)
+        total = msg[cell]
         for b in range(levels):
-            both = acc[b * slots : (b + 1) * slots] + part[b * slots : (b + 1) * slots]
-            total = total + both * wb_ref[b : b + 1]
-        msg[cell] = total.astype(jnp.bfloat16)
+            total = total + part[b * slots : (b + 1) * slots] * wb[b : b + 1]
+        msg[cell] = total
+
+    def halo_in(keys):
+        for key in keys:
+            halo[key].wait()
+            side[key].start()
+
+    def side_in(keys):
+        for key in keys:
+            side[key].wait()
+
+    side_in([(0, 0)])
+    weigh(0, jnp.int32(0))
+
+    ends = 2 * cy - 4
+    events = [
+        (0, sum_pair),
+        (ends - 2, lambda: halo_in([(0, -1)])),
+        (ends - 1, lambda: side_in([(0, -1)])),
+        (ends, lambda: halo_in([(0, 1)])),
+        (ends + 1, lambda: side_in([(0, 1)])),
+        (ends + 2, lambda: halo_in([(1, 0), (-1, 0)])),
+        (ends + 2, filter_share),
+        (ends + 3, lambda: side_in([(1, 0), (-1, 0)])),
+        (3 * cy - 4, lambda: halo_in([(1, -1), (-1, -1)])),
+        (3 * cy - 3, lambda: side_in([(1, -1), (-1, -1)])),
+        (3 * cy - 3, lambda: halo_in([(1, 1), (-1, 1)])),
+        (3 * cy - 2, lambda: side_in([(1, 1), (-1, 1)])),
+        (3 * cy - 1, join_field),
+    ]
+
+    @pl.loop(0, 3 * cy)
+    def _(j):
+        for when, what in events:
+            pl.when(j == when)(what)
+        weigh(1, j)
+        gather(0, j)
+        weigh(0, j + 1)
+        gather(1, j)
 
     field_copy(core).wait_send()
     field_copy(1 - core).wait_recv()
@@ -358,11 +436,34 @@
         far = lax.dot_general(
             basis[:, lanes], waves_field, (((0,), (0,)), ((), ())), preferred_element_type=jnp.float32
         )
-        joined = far + jnp.dot(msg[cell], wm_ref[...], preferred_element_type=jnp.float32)
+        near = msg[cell].astype(jnp.bfloat16)
+        joined = far + jnp.dot(near, wm_ref[...], preferred_element_type=jnp.float32)
         hidden = (joined / (1.0 + jnp.exp(-joined))).astype(jnp.bfloat16)
-        atom = pack_ref[cell // cy, cell % cy, 0:slots].astype(jnp.float32)
-        result = atom + jnp.dot(hidden, wo_ref[...], preferred_element_type=jnp.float32)
-        out_ref[cell] = (result * home_ref[cell, :, 3:4]).astype(jnp.bfloat16)
+        atom = wide[1 + cell // cy, 1 + cell % cy, 0, 0:slots].astype(jnp.float32)
+        result = jnp.dot(hidden, wo_ref[...], preferred_element_type=jnp.float32)
+        there = out_mask[cell]
+        out_ref[cell] = (atom + result * there).astype(jnp.bfloat16)
+
+
+def radial_chain(gx, gy, gz, levels, diagonal, p0, phi, slots):
+    rows = gx.shape[0]
+    sq = jnp.minimum(gx * gx + gy * gy + gz * gz, 1.0)
+    dist = sq * lax.rsqrt(jnp.maximum(sq, 1e-30))
+    ratio = jnp.exp2(dist * (2.0 * sharpness / (levels - 1) * math.log2(math.e)))
+    edge = 1.0 - sq
+    val = edge * edge * jnp.exp2(sq * (-sharpness * math.log2(math.e)))
+    if diagonal is not None:
+        row = lax.broadcasted_iota(jnp.int32, val.shape, 0) + diagonal
+        lane = lax.broadcasted_iota(jnp.int32, val.shape, 1)
+        val = jnp.where(row == lane, 0.0, val)
+    second = ratio * ratio
+    steps = [val.astype(jnp.bfloat16), (val * ratio).astype(jnp.bfloat16)]
+    fourth = (second * second).astype(jnp.bfloat16)
+    second = second.astype(jnp.bfloat16)
+    for b in range(2, levels):
+        steps.append(steps[b - 2] * second if b < 4 else steps[b - 4] * fourth)
+    for b in range(levels):
+        phi[b * slots + p0 : b * slots + p0 + rows] = steps[b]
 
 
 def radial_terms(gx, gy, gz, levels, center, p0, phi, col, slots):
@@ -403,6 +504,62 @@
     full = lambda shape: pl.BlockSpec(shape, lambda i: (0,) * len(shape))
     params = pltpu.CompilerParams(dimension_semantics=("arbitrary",), vmem_limit_bytes=56 * 2**20)
 
+    fold_z = grid[2] == 2 and cz == 1
+    counts = tuple(lax.axis_size(n) for n in axes)
+    rows = waves // devices
+    chips = counts[0] * counts[1]
+    if fold_z and rows % 16 == 0 and min(counts) > 1 and cx == 2 and cy > 2 and 4 * cells <= slots == 128:
+        vmem = pl.BlockSpec(memory_space=pltpu.VMEM)
+        dma = pltpu.SemaphoreType.DMA
+        out = pl.pallas_call(
+            functools.partial(layer_kernel, counts, levels),
+            in_specs=[vmem] * 9,
+            out_specs=vmem,
+            out_shape=jax.ShapeDtypeStruct((cells, slots, feat), jnp.bfloat16),
+            scratch_shapes=[
+                pltpu.VMEM((cx + 2, cy + 2, 2, slots + 8, feat), jnp.bfloat16),
+                pltpu.VMEM((slots, slots), jnp.float32),
+                pltpu.VMEM((cells, slots, feat), jnp.float32),
+                pltpu.VMEM((waves, 8), jnp.float32),
+                pltpu.VMEM((levels, feat), jnp.float32),
+                pltpu.VMEM((cells, 3, slots, slots), jnp.float32),
+                pltpu.VMEM((2, 6, levels * slots, slots), jnp.bfloat16),
+                pltpu.VMEM((cells, slots, feat), jnp.float32),
+                pltpu.VMEM((2 * waves, cells * slots), jnp.bfloat16),
+                pltpu.VMEM((2, chips, 2, rows, feat), jnp.bfloat16),
+                pltpu.VMEM((2, chips, rows, feat), jnp.bfloat16),
+                pltpu.VMEM((2, chips, rows, feat), jnp.bfloat16),
+                pltpu.VMEM((chips, 2, rows, feat), jnp.bfloat16),
+                pltpu.VMEM((2, rows, feat), jnp.bfloat16),
+                pltpu.VMEM((2, chips, 2, rows, feat), jnp.bfloat16),
+                dma((8,)),
+                dma((8,)),
+                dma((9,)),
+                dma((9,)),
+                dma((2,)),
+                dma((2,)),
+                dma((chips,)),
+                dma((chips,)),
+                dma((chips,)),
+                dma((chips,)),
+            ],
+            compiler_params=pltpu.CompilerParams(
+                collective_id=0, has_side_effects=True, vmem_limit_bytes=56 * 2**20
+            ),
+            name="layer",
+        )(
+            features.reshape(cx, cy, slots, feat),
+            fractions.transpose(0, 2, 3, 1, 4).reshape(cx, 3, cy, slots),
+            occupied.reshape(cells, slots),
+            wave_index,
+            radial_weight.T,
+            ewald_mix,
+            ewald_weight,
+            msg_weight,
+            out_weight,
+        )
+        return out.reshape(features.shape)
+
     masked = features * occupied[..., None].astype(jnp.bfloat16)
     frac = fractions.astype(jnp.float32)
     cell_feat = masked.reshape(cells, slots, feat)
@@ -427,57 +584,9 @@
     )
     wave_turn = (index / lengths[:, None]).T
 
-    fold_z = grid[2] == 2 and cz == 1
     level = jnp.arange(levels, dtype=jnp.float32) / (levels - 1)
     wb = radial_weight * (jnp.exp(-sharpness * level * level) / math.sqrt(4.0 * slots))[:, None]
     wb = jnp.repeat(wb, feat // heads, axis=1)
-    counts = tuple(lax.axis_size(n) for n in axes)
-    rows = waves // devices
-    chips = counts[0] * counts[1]
-    if fold_z and rows % 16 == 0 and min(counts) > 1:
-        spread = jnp.pad(fractions, ((0, 0),) * 3 + ((0, 13), (0, feat - slots)))
-        pack = jnp.concatenate([masked, spread], axis=3).reshape(cx, cy, slots + 16, feat)
-        damp = lax.dynamic_slice_in_dim(damping, lax.axis_index(axes) * rows, rows, 0)
-        damp = jnp.concatenate([damp, damp]).reshape(2 * rows, 1)
-        vmem = pl.BlockSpec(memory_space=pltpu.VMEM)
-        dma = pltpu.SemaphoreType.DMA
-        out = pl.pallas_call(
-            functools.partial(layer_kernel, counts, levels),
-            in_specs=[vmem] * 10,
-            out_specs=vmem,
-            out_shape=jax.ShapeDtypeStruct((cells, slots, feat), jnp.bfloat16),
-            scratch_shapes=[
-                pltpu.VMEM((cx + 2, cy + 2, 2, slots + 16, feat), jnp.bfloat16),
-                pltpu.VMEM((3, slots, slots), jnp.float32),
-                pltpu.VMEM((3, levels * slots, 6 * slots), jnp.bfloat16),
-                pltpu.VMEM((levels * slots, feat), jnp.float32),
-                pltpu.VMEM((2 * waves, cells * slots), jnp.bfloat16),
-                pltpu.VMEM((2, chips, 2, rows, feat), jnp.bfloat16),
-                pltpu.VMEM((2, chips, rows, feat), jnp.bfloat16),
-                pltpu.VMEM((2, chips, rows, feat), jnp.bfloat16),
-                pltpu.VMEM((chips, 2, rows, feat), jnp.bfloat16),
-                pltpu.VMEM((2, rows, feat), jnp.bfloat16),
-                pltpu.VMEM((2, chips, 2, rows, feat), jnp.bfloat16),
-                pltpu.VMEM((cells, slots, feat), jnp.bfloat16),
-                dma((8,)),
-                dma((8,)),
-                dma((9,)),
-                dma((9,)),
-                dma,
-                dma((2,)),
-                dma((2,)),
-                dma((chips,)),
-                dma((chips,)),
-                dma((chips,)),
-                dma((chips,)),
-            ],
-            compiler_params=pltpu.CompilerParams(
-                collective_id=0, has_side_effects=True, vmem_limit_bytes=56 * 2**20
-            ),
-            name="layer",
-        )(pack, home, pos, wave_turn, wb, damp, ewald_mix, ewald_weight, msg_weight, out_weight)
-        return out.reshape(features.shape)
-
     basis, struct = pl.pallas_call(
         basis_kernel,
         grid=(cells,),

time: 64.8 us -> 48.2 us (0.74)
  Pallas kernels: 53.7 us -> 46.1 us
  other arithmetic: 4.6 us -> 0 us
  local copies, waits for them, and re-layouts: 6.14 us -> 1.87 us
    pallas_call x1, Pallas kernels: 53.7 us -> 46.1 us  [body(): pl.pallas_call(functools.partial(layer_kernel, counts, levels), in_specs=...]
    reshape x2 -> x0, local copies, waits for them, and re-layouts: 1.37 us -> none  [the longest x1 0.69 us: body(): damp = jnp.concatenate([damp, damp]).reshape(2 * rows, 1)]
    mul x3 -> x0, other arithmetic: 1.26 us -> none  [the longest x1 1.24 us: body(): masked = features * occupied[..., None].astype(jnp.bfloat16)]
    concatenate x1 -> x0, local copies, waits for them, and re-layouts: 1.03 us -> none  [body(): jnp.concatenate([frac, occupied[:, :, :, None, :].astype(jnp.float32)], a...]
    reshape x2 -> x0, other arithmetic: 0.93 us -> none  [the longest x1 0.85 us: body(): jnp.concatenate([masked, spread], axis=3).reshape(cx, cy, slots + 16, feat)]
    div x1 -> x0, local copies, waits for them, and re-layouts: 0.85 us -> none  [body(): wave_turn = (index / lengths[:, None]).T]
    add x2 -> x0, other arithmetic: 0.84 us -> none  [body(): pos = (origin + frac).reshape(cells, 3, slots)]
    reduce_sum x1 -> x0, other arithmetic: 0.78 us -> none  [body(): wave_sq = jnp.sum(wave_vec * wave_vec, axis=0)]
where the time goes in v1:
time: 48.2 us; the launch traced here: 48 us
  Pallas kernels  46.1 us (96%)
  local copies, waits for them, and re-layouts  1.87 us (4%)
    pallas_call x1, Pallas kernels, body(): pl.pallas_call(functools.partial(layer_kernel, counts, levels), in_specs=...  46.1 us
    unnamed x1, local copies, waits for them, and re-layouts  1.87 us

profile of v1, /device:TPU:0, one launch (start us, length us, event | category | flops | bytes accessed | tf_op | source)
XLA Modules:
  0.0 48.0 jit_solution(4782210522599236105)
XLA Ops:
  0.0 46.1 %layer.1 = bf16[8,128,256]{2,1,0:T(8,128)(2,1)} custom-call(bf16[2,4,128,256]{3,2,1,0:T(8,128)(2,1)} %bitcast.12, bf16[2,3,4,128]{3,2,1,0:T(4,128)(2,1)} %bitcast.13, s32[8,128]{1,0:T(8,128)} %bitcast.14, s32[3,512]{1,0:T(4,128)} %index_ref.1, f32[4,8]{1,0:T(4,128)} %bitcast.15, f32[256,256]{1,0:T(8,128)} %mix_ref.1, bf16[256,256]{1,0:T(8,128)(2,1)} %we_ref.1, ...), custom_call_target="tpu_custom_call" | custom-call | tf_op jit(solution)/shard_map/layer/pallas_call | solution.py:514
  46.1 1.9 %copy.13 = bf16[2,4,1,128,256]{4,3,2,1,0:T(8,128)(2,1)} copy(bf16[2,4,1,128,256]{4,3,2,1,0:T(8,128)(2,1)} %bitcast.11) | data formatting | bytes 1048576

commit v2 on v1

--- a/solution.py
+++ b/solution.py
@@ -123,6 +123,16 @@
 def layer_kernel(
     counts,
     levels,
+    feat_in,
+    frac_in,
+    occ_in,
+    index_in,
+    radial_in,
+    mix_in,
+    we_in,
+    wm_in,
+    wo_in,
+    out_ref,
     feat_ref,
     frac_ref,
     occ_ref,
@@ -132,7 +142,7 @@
     we_ref,
     wm_ref,
     wo_ref,
-    out_ref,
+    in_sem,
     wide,
     rows_sc,
     out_mask,
@@ -173,6 +183,7 @@
     mesh_id = pl.DeviceIdType.MESH
     pad = wide.shape[3] - slots
 
+    reach = 2.0 * sharpness / (levels - 1) * math.log2(math.e)
     partner = (at[0], at[1], 1 - core)
 
     def same_core(k):
@@ -184,6 +195,12 @@
             src_ref=src, dst_ref=dst, send_sem=send, recv_sem=recv, device_id=partner, device_id_type=mesh_id
         )
 
+    sources = [frac_in, occ_in, index_in, radial_in, feat_in, mix_in, we_in, wm_in, wo_in]
+    places = [frac_ref, occ_ref, index_ref, radial_ref, feat_ref, mix_ref, we_ref, wm_ref, wo_ref]
+    loads = [pltpu.make_async_copy(src, dst, in_sem.at[n]) for n, (src, dst) in enumerate(zip(sources, places))]
+    for load in loads:
+        load.start()
+
     barrier = pltpu.get_barrier_semaphore()
 
     @pl.loop(1, chips)
@@ -192,6 +209,8 @@
 
     pl.semaphore_signal(barrier, inc=1, device_id=partner, device_id_type=mesh_id)
 
+    for load in loads[:4]:
+        load.wait()
     rows_sc[...] = jnp.zeros_like(rows_sc)
     for x in range(cx):
         for a in range(3):
@@ -201,49 +220,9 @@
     turned = rows_sc[...].T
     for x in range(cx):
         for y in range(cy):
-            cell = x * cy + y
-            ks = [(x * 3 + a) * cy + y for a in range(3)]
-            there = jnp.broadcast_to(turned[:, 3 * cells + cell : 3 * cells + cell + 1], (slots, feat))
-            wide[1 + x, 1 + y, 0, 0:slots] = feat_ref[x, y] * there.astype(jnp.bfloat16)
-            own = jnp.concatenate([rows_sc[k : k + 1] for k in ks] + [jnp.zeros((pad - 3, slots), jnp.float32)])
-            own = jnp.concatenate([own, jnp.zeros((pad, feat - slots), jnp.float32)], axis=1)
-            wide[1 + x, 1 + y, 0, slots:] = own.astype(jnp.bfloat16)
-
-    pl.semaphore_wait(barrier, chips)
-
-    def span(step, length):
-        if step == 0:
-            return 1, 1, length
-        if step == 1:
-            return length, 0, 1
-        return 1, length + 1, 1
-
-    halo, side = {}, {}
-    for n, (dx, dy) in enumerate([(0, 1), (0, -1), (1, 0), (-1, 0), (1, 1), (1, -1), (-1, 1), (-1, -1), (0, 0)]):
-        sx, tx, lx = span(dx, cx)
-        sy, ty, ly = span(dy, cy)
-        region = (pl.ds(tx, lx), pl.ds(ty, ly))
-        side[dx, dy] = to_partner(wide.at[(*region, 0)], wide.at[(*region, 1)], side_send.at[n], side_recv.at[n])
-        if (dx, dy) == (0, 0):
-            continue
-        target = ((at[0] + dx + counts[0]) % counts[0], (at[1] + dy + counts[1]) % counts[1], core)
-        halo[dx, dy] = pltpu.make_async_remote_copy(
-            src_ref=wide.at[pl.ds(sx, lx), pl.ds(sy, ly), 0],
-            dst_ref=wide.at[(*region, 0)],
-            send_sem=halo_send.at[n],
-            recv_sem=halo_recv.at[n],
-            device_id=target,
-            device_id_type=mesh_id,
-        )
-    side[0, 0].start()
-    for copy in halo.values():
-        copy.start()
-
-    for x in range(cx):
-        for y in range(cy):
             for a in range(3):
                 k = (x * 3 + a) * cy + y
-                hb[x * cy + y, a] = jnp.broadcast_to(turned[:, k : k + 1], (slots, slots))
+                hb[x * cy + y, a] = jnp.broadcast_to(turned[:, k : k + 1] * reach, (slots, slots))
             k = 3 * cells + x * cy + y
             out_mask[x * cy + y] = jnp.broadcast_to(turned[:, k : k + 1], (slots, feat))
     for w0 in range(0, waves, 128):
@@ -254,9 +233,19 @@
     mine = owner == lax.broadcasted_iota(jnp.int32, (heads, feat), 0)
     for b in range(levels):
         level = b / (levels - 1)
-        scale = math.exp(-sharpness * level * level) / math.sqrt(4.0 * slots)
+        scale = math.exp(-sharpness * level * level) / math.sqrt(4.0 * slots) / reach**4
         column = jnp.broadcast_to(radial_ref[:, b : b + 1], (heads, feat)) * scale
         wb[b : b + 1] = jnp.sum(jnp.where(mine, column, 0.0), axis=0, keepdims=True)
+
+    loads[4].wait()
+    for x in range(cx):
+        for y in range(cy):
+            cell = x * cy + y
+            ks = [(x * 3 + a) * cy + y for a in range(3)]
+            wide[1 + x, 1 + y, 0, 0:slots] = feat_ref[x, y] * out_mask[cell].astype(jnp.bfloat16)
+            own = jnp.concatenate([rows_sc[k : k + 1] for k in ks] + [jnp.zeros((pad - 3, slots), jnp.float32)])
+            own = jnp.concatenate([own, jnp.zeros((pad, feat - slots), jnp.float32)], axis=1)
+            wide[1 + x, 1 + y, 0, slots:] = own.astype(jnp.bfloat16)
 
     @pl.loop(0, cells)
     def _(cell):
@@ -283,8 +272,40 @@
         .astype(jnp.bfloat16)
         .reshape(2, chips, 2, rows, feat)
     )
+    pl.semaphore_wait(barrier, chips)
+
+    def span(step, length):
+        if step == 0:
+            return 1, 1, length
+        if step == 1:
+            return length, 0, 1
+        return 1, length + 1, 1
+
+    halo, side = {}, {}
+    for n, (dx, dy) in enumerate([(0, 1), (0, -1), (1, 0), (-1, 0), (1, 1), (1, -1), (-1, 1), (-1, -1), (0, 0)]):
+        sx, tx, lx = span(dx, cx)
+        sy, ty, ly = span(dy, cy)
+        region = (pl.ds(tx, lx), pl.ds(ty, ly))
+        side[dx, dy] = to_partner(wide.at[(*region, 0)], wide.at[(*region, 1)], side_send.at[n], side_recv.at[n])
+        if (dx, dy) == (0, 0):
+            continue
+        target = ((at[0] + dx + counts[0]) % counts[0], (at[1] + dy + counts[1]) % counts[1], core)
+        halo[dx, dy] = pltpu.make_async_remote_copy(
+            src_ref=wide.at[pl.ds(sx, lx), pl.ds(sy, ly), 0],
+            dst_ref=wide.at[(*region, 0)],
+            send_sem=halo_send.at[n],
+            recv_sem=halo_recv.at[n],
+            device_id=target,
+            device_id_type=mesh_id,
+        )
+
     swap = to_partner(struct.at[:, :, 1 - core], pair, pair_send.at[0], pair_recv.at[0])
     swap.start()
+    side[0, 0].start()
+    for copy in halo.values():
+        copy.start()
+    for load in loads[5:]:
+        load.wait()
     msg[...] = jnp.zeros_like(msg)
 
     def part_copy(k):
@@ -359,28 +380,28 @@
         xi, y = place(x, j)
         cell = x * cy + y
         step = xi - (x + 1)
-        chunk = 32
+        chunk = 16
         for oy in range(3):
-            for oz in range(2):
-                g = wide[xi, y + oy, oz, slots : slots + pad, 0:slots].astype(jnp.float32)
-                nx = g[0:1] + step.astype(jnp.float32)
-                ny = g[1:2] + (oy - 1.0)
-                nz = g[2:3]
-                col = oy * 2 + oz
-                for p0 in range(0, slots, chunk):
-                    gx = nx - hb[cell, 0, p0 : p0 + chunk]
-                    gy = ny - hb[cell, 1, p0 : p0 + chunk]
-                    gz = nz - hb[cell, 2, p0 : p0 + chunk]
-                    if oz == 1:
-                        gz = 1.0 - jnp.abs(gz)
-                    diagonal = p0 + step * slots if (oy, oz) == (1, 0) else None
-                    radial_chain(gx, gy, gz, levels, diagonal, p0, phi.at[x, col], slots)
+            near = [
+                wide[xi, y + oy, oz, slots : slots + pad, 0:slots].astype(jnp.float32) * reach for oz in range(2)
+            ]
+            near = jnp.concatenate(near, axis=1)
+            nx = near[0:1] + step.astype(jnp.float32) * reach
+            ny = near[1:2] + (oy - 1.0) * reach
+            nz = near[2:3]
+            for p0 in range(0, slots, chunk):
+                gx, gy, gz = (
+                    n - jnp.concatenate([hb[cell, a, p0 : p0 + chunk]] * 2, axis=1) for a, n in enumerate((nx, ny, nz))
+                )
+                gz = jnp.concatenate([gz[:, :slots], reach - jnp.abs(gz[:, slots:])], axis=1)
+                diagonal = p0 + step * slots if oy == 1 else None
+                radial_chain(gx, gy, gz, levels, reach, diagonal, p0, phi.at[x, oy], slots)
 
     def gather(x, j):
         xi, y = place(x, j)
         cell = x * cy + y
         near = wide[xi, pl.ds(y, 3), :, 0:slots].reshape(6 * slots, feat)
-        left = jnp.concatenate([phi[x, col] for col in range(6)], axis=1)
+        left = jnp.concatenate([phi[x, oy] for oy in range(3)], axis=1)
         part = jnp.dot(left, near, preferred_element_type=jnp.float32)
         total = msg[cell]
         for b in range(levels):
@@ -445,17 +466,16 @@
         out_ref[cell] = (atom + result * there).astype(jnp.bfloat16)
 
 
-def radial_chain(gx, gy, gz, levels, diagonal, p0, phi, slots):
+def radial_chain(gx, gy, gz, levels, reach, diagonal, p0, phi, slots):
     rows = gx.shape[0]
-    sq = jnp.minimum(gx * gx + gy * gy + gz * gz, 1.0)
-    dist = sq * lax.rsqrt(jnp.maximum(sq, 1e-30))
-    ratio = jnp.exp2(dist * (2.0 * sharpness / (levels - 1) * math.log2(math.e)))
-    edge = 1.0 - sq
-    val = edge * edge * jnp.exp2(sq * (-sharpness * math.log2(math.e)))
+    sq = jnp.minimum(gx * gx + gy * gy + gz * gz, reach * reach)
+    ratio = jnp.exp2(sq * lax.rsqrt(jnp.maximum(sq, 1e-30)))
+    edge = reach * reach - sq
+    val = edge * edge * jnp.exp2(sq * (-sharpness * math.log2(math.e) / reach**2))
     if diagonal is not None:
-        row = lax.broadcasted_iota(jnp.int32, val.shape, 0) + diagonal
-        lane = lax.broadcasted_iota(jnp.int32, val.shape, 1)
-        val = jnp.where(row == lane, 0.0, val)
+        row = lax.broadcasted_iota(jnp.int32, (rows, slots), 0) + diagonal
+        lane = lax.broadcasted_iota(jnp.int32, (rows, slots), 1)
+        val = jnp.concatenate([jnp.where(row == lane, 0.0, val[:, :slots]), val[:, slots:]], axis=1)
     second = ratio * ratio
     steps = [val.astype(jnp.bfloat16), (val * ratio).astype(jnp.bfloat16)]
     fourth = (second * second).astype(jnp.bfloat16)
@@ -513,17 +533,27 @@
         dma = pltpu.SemaphoreType.DMA
         out = pl.pallas_call(
             functools.partial(layer_kernel, counts, levels),
-            in_specs=[vmem] * 9,
+            in_specs=[pl.BlockSpec(memory_space=pl.ANY)] * 9,
             out_specs=vmem,
-            out_shape=jax.ShapeDtypeStruct((cells, slots, feat), jnp.bfloat16),
+            out_shape=pltpu.VMEM((cells, slots, feat), jnp.bfloat16),
             scratch_shapes=[
+                pltpu.VMEM((cx, cy, slots, feat), jnp.bfloat16),
+                pltpu.VMEM((cx, 3, cy, slots), jnp.bfloat16),
+                pltpu.VMEM((cells, slots), jnp.int32),
+                pltpu.VMEM(wave_index.shape, jnp.int32),
+                pltpu.VMEM((heads, levels), jnp.float32),
+                pltpu.VMEM(ewald_mix.shape, jnp.float32),
+                pltpu.VMEM(ewald_weight.shape, jnp.bfloat16),
+                pltpu.VMEM(msg_weight.shape, jnp.bfloat16),
+                pltpu.VMEM(out_weight.shape, jnp.bfloat16),
+                dma((9,)),
                 pltpu.VMEM((cx + 2, cy + 2, 2, slots + 8, feat), jnp.bfloat16),
                 pltpu.VMEM((slots, slots), jnp.float32),
                 pltpu.VMEM((cells, slots, feat), jnp.float32),
                 pltpu.VMEM((waves, 8), jnp.float32),
                 pltpu.VMEM((levels, feat), jnp.float32),
                 pltpu.VMEM((cells, 3, slots, slots), jnp.float32),
-                pltpu.VMEM((2, 6, levels * slots, slots), jnp.bfloat16),
+                pltpu.VMEM((2, 3, levels * slots, 2 * slots), jnp.bfloat16),
                 pltpu.VMEM((cells, slots, feat), jnp.float32),
                 pltpu.VMEM((2 * waves, cells * slots), jnp.bfloat16),
                 pltpu.VMEM((2, chips, 2, rows, feat), jnp.bfloat16),

time: 48.2 us -> 48.7 us (1.010)
  Pallas kernels: 46.1 us -> 47.8 us
  local copies, waits for them, and re-layouts: 1.87 us -> 0.8 us
    pallas_call x1, Pallas kernels: 46.1 us -> 47.8 us  [body(): pl.pallas_call(functools.partial(layer_kernel, counts, levels), in_specs=...]
    unnamed x1, local copies, waits for them, and re-layouts: 1.87 us -> 0.8 us
where the time goes in v2:
time: 48.7 us; the launch traced here: 48.6 us
  Pallas kernels  47.8 us (98%)
  local copies, waits for them, and re-layouts  0.8 us (2%)
    pallas_call x1, Pallas kernels, body(): pl.pallas_call(functools.partial(layer_kernel, counts, levels), in_specs=...  47.8 us

profile of v2, /device:TPU:0, one launch (start us, length us, event | category | flops | bytes accessed | tf_op | source)
XLA Modules:
  0.0 48.6 jit_solution(17645220967317279063)
XLA Ops:
  0.0 47.8 %layer.1 = bf16[8,128,256]{2,1,0:T(8,128)(2,1)S(1)} custom-call(bf16[2,4,128,256]{3,2,1,0:T(8,128)(2,1)} %bitcast.12, bf16[2,3,4,128]{3,2,1,0:T(4,128)(2,1)} %bitcast.13, s32[8,128]{1,0:T(8,128)} %bitcast.14, s32[3,512]{1,0:T(4,128)} %index_in.1, f32[4,8]{1,0:T(4,128)} %bitcast.15, f32[256,256]{1,0:T(8,128)} %mix_in.1, bf16[256,256]{1,0:T(8,128)(2,1)} %we_in.1, ...), custom_call_target="tpu_custom_call" | custom-call | tf_op jit(solution)/shard_map/layer/pallas_call | solution.py:534
  47.8 0.8 %copy.13 = bf16[2,4,1,128,256]{4,3,2,1,0:T(8,128)(2,1)} copy(bf16[2,4,1,128,256]{4,3,2,1,0:T(8,128)(2,1)S(1)} %bitcast.11) | data formatting | bytes 1048576

commit v3 on v2

--- a/solution.py
+++ b/solution.py
@@ -156,8 +156,9 @@
     pair,
     chip_sum,
     parts,
-    share,
+    lines,
     field,
+    token,
     halo_send,
     halo_recv,
     side_send,
@@ -166,6 +167,8 @@
     pair_recv,
     part_send,
     part_recv,
+    line_send,
+    line_recv,
     share_send,
     share_recv,
 ):
@@ -177,18 +180,20 @@
     grid = (counts[0] * cx, counts[1] * cy, counts[2])
     rows = waves // devices
     at = (lax.axis_index("gx"), lax.axis_index("gy"), lax.axis_index("gz"))
-    chips = counts[0] * counts[1]
-    chip = at[0] * counts[1] + at[1]
     core = at[2]
+    nx, ny = counts[0], counts[1]
     mesh_id = pl.DeviceIdType.MESH
     pad = wide.shape[3] - slots
-
     reach = 2.0 * sharpness / (levels - 1) * math.log2(math.e)
     partner = (at[0], at[1], 1 - core)
-
-    def same_core(k):
-        peer = (chip + k) % chips
-        return (peer // counts[1], peer % counts[1], core)
+    lower = (at[0] + nx - 1) // nx
+    upper = (2 * nx - 2 - at[0]) // nx
+
+    def over_x(k):
+        return ((at[0] + k + nx) % nx, at[1], core)
+
+    def over_y(k):
+        return (at[0], (at[1] + k + ny) % ny, core)
 
     def to_partner(src, dst, send, recv):
         return pltpu.make_async_remote_copy(
@@ -203,11 +208,19 @@
 
     barrier = pltpu.get_barrier_semaphore()
 
-    @pl.loop(1, chips)
-    def _(k):
-        pl.semaphore_signal(barrier, inc=1, device_id=same_core(k), device_id_type=mesh_id)
+    def greet_line(sem):
+        @pl.when(at[0] > 0)
+        def _():
+            pl.semaphore_signal(sem, inc=1, device_id=over_x(-1), device_id_type=mesh_id)
+
+        @pl.when(at[0] < nx - 1)
+        def _():
+            pl.semaphore_signal(sem, inc=1, device_id=over_x(1), device_id_type=mesh_id)
 
     pl.semaphore_signal(barrier, inc=1, device_id=partner, device_id_type=mesh_id)
+    greet_line(barrier)
+    for k in range(1, ny):
+        pl.semaphore_signal(barrier, inc=1, device_id=over_y(k), device_id_type=mesh_id)
 
     for load in loads[:4]:
         load.wait()
@@ -220,11 +233,67 @@
     turned = rows_sc[...].T
     for x in range(cx):
         for y in range(cy):
+            k = 3 * cells + x * cy + y
+            out_mask[x * cy + y] = jnp.broadcast_to(turned[:, k : k + 1], (slots, feat))
+    loads[4].wait()
+    for x in range(cx):
+        for y in range(cy):
+            cell = x * cy + y
+            ks = [(x * 3 + a) * cy + y for a in range(3)]
+            wide[1 + x, 1 + y, 0, 0:slots] = feat_ref[x, y] * out_mask[cell].astype(jnp.bfloat16)
+            own = jnp.concatenate([rows_sc[k : k + 1] for k in ks] + [jnp.zeros((pad - 3, slots), jnp.float32)])
+            own = jnp.concatenate([own, jnp.zeros((pad, feat - slots), jnp.float32)], axis=1)
+            wide[1 + x, 1 + y, 0, slots:] = own.astype(jnp.bfloat16)
+
+    def span(step, length):
+        if step == 0:
+            return 1, 1, length
+        if step == 1:
+            return length, 0, 1
+        return 1, length + 1, 1
+
+    halo, side = {}, {}
+    for n, (dx, dy) in enumerate([(0, 1), (0, -1), (1, 0), (-1, 0), (1, 1), (1, -1), (-1, 1), (-1, -1), (0, 0)]):
+        sx, tx, lx = span(dx, cx)
+        sy, ty, ly = span(dy, cy)
+        region = (pl.ds(tx, lx), pl.ds(ty, ly))
+        side[dx, dy] = to_partner(wide.at[(*region, 0)], wide.at[(*region, 1)], side_send.at[n], side_recv.at[n])
+        if (dx, dy) == (0, 0):
+            continue
+        halo[dx, dy] = pltpu.make_async_remote_copy(
+            src_ref=wide.at[pl.ds(tx if dx and dy else sx, lx), pl.ds(sy, ly), 0],
+            dst_ref=wide.at[(*region, 0)],
+            send_sem=halo_send.at[n],
+            recv_sem=halo_recv.at[n],
+            device_id=over_y(dy) if dy else over_x(dx),
+            device_id_type=mesh_id,
+        )
+
+    def send_faces(direct):
+        for step, inside in ((1, at[0] < nx - 1), (-1, at[0] > 0)):
+            pl.when(inside if direct else jnp.logical_not(inside))(halo[step, 0].start)
+
+    def open_links():
+        pl.semaphore_wait(barrier, 1 + lower + upper + ny - 1)
+        greet_line(token.at[0])
+        side[0, 0].start()
+        halo[0, 1].start()
+        halo[0, -1].start()
+        send_faces(True)
+
+    def pass_token():
+        pl.semaphore_wait(token.at[0], lower + upper)
+        greet_line(token.at[1])
+
+    def open_wrap():
+        pl.semaphore_wait(token.at[1], lower + upper)
+        send_faces(False)
+
+    for x in range(cx):
+        for y in range(cy):
             for a in range(3):
                 k = (x * 3 + a) * cy + y
                 hb[x * cy + y, a] = jnp.broadcast_to(turned[:, k : k + 1] * reach, (slots, slots))
-            k = 3 * cells + x * cy + y
-            out_mask[x * cy + y] = jnp.broadcast_to(turned[:, k : k + 1], (slots, feat))
     for w0 in range(0, waves, 128):
         part = [index_ref[a : a + 1, w0 : w0 + 128].astype(jnp.float32) * (1.0 / grid[a]) for a in range(3)]
         part = jnp.concatenate(part + [jnp.zeros((5, 128), jnp.float32)])
@@ -237,16 +306,6 @@
         column = jnp.broadcast_to(radial_ref[:, b : b + 1], (heads, feat)) * scale
         wb[b : b + 1] = jnp.sum(jnp.where(mine, column, 0.0), axis=0, keepdims=True)
 
-    loads[4].wait()
-    for x in range(cx):
-        for y in range(cy):
-            cell = x * cy + y
-            ks = [(x * 3 + a) * cy + y for a in range(3)]
-            wide[1 + x, 1 + y, 0, 0:slots] = feat_ref[x, y] * out_mask[cell].astype(jnp.bfloat16)
-            own = jnp.concatenate([rows_sc[k : k + 1] for k in ks] + [jnp.zeros((pad - 3, slots), jnp.float32)])
-            own = jnp.concatenate([own, jnp.zeros((pad, feat - slots), jnp.float32)], axis=1)
-            wide[1 + x, 1 + y, 0, slots:] = own.astype(jnp.bfloat16)
-
     @pl.loop(0, cells)
     def _(cell):
         x = cell // cy
@@ -255,6 +314,9 @@
         start = [(at[0] * cx + x).astype(jnp.float32), (at[1] * cy + y).astype(jnp.float32), core.astype(jnp.float32)]
         pos = [rows_sc[pl.ds(first + a * cy, 1)] + start[a] for a in range(3)]
         lanes = pl.ds(pl.multiple_of(cell * slots, slots), slots)
+        pl.when(cell == 0)(open_links)
+        pl.when(cell == cells // 4)(pass_token)
+        pl.when(cell == cells // 2 + 1)(open_wrap)
         chunk = 64
         for w0 in range(0, waves, chunk):
             wv = turn_cols[w0 : w0 + chunk]
@@ -270,104 +332,82 @@
     struct[...] = (
         jnp.dot(basis[...], atoms, preferred_element_type=jnp.float32)
         .astype(jnp.bfloat16)
-        .reshape(2, chips, 2, rows, feat)
+        .reshape(struct.shape)
     )
-    pl.semaphore_wait(barrier, chips)
-
-    def span(step, length):
-        if step == 0:
-            return 1, 1, length
-        if step == 1:
-            return length, 0, 1
-        return 1, length + 1, 1
-
-    halo, side = {}, {}
-    for n, (dx, dy) in enumerate([(0, 1), (0, -1), (1, 0), (-1, 0), (1, 1), (1, -1), (-1, 1), (-1, -1), (0, 0)]):
-        sx, tx, lx = span(dx, cx)
-        sy, ty, ly = span(dy, cy)
-        region = (pl.ds(tx, lx), pl.ds(ty, ly))
-        side[dx, dy] = to_partner(wide.at[(*region, 0)], wide.at[(*region, 1)], side_send.at[n], side_recv.at[n])
-        if (dx, dy) == (0, 0):
-            continue
-        target = ((at[0] + dx + counts[0]) % counts[0], (at[1] + dy + counts[1]) % counts[1], core)
-        halo[dx, dy] = pltpu.make_async_remote_copy(
-            src_ref=wide.at[pl.ds(sx, lx), pl.ds(sy, ly), 0],
-            dst_ref=wide.at[(*region, 0)],
-            send_sem=halo_send.at[n],
-            recv_sem=halo_recv.at[n],
-            device_id=target,
-            device_id_type=mesh_id,
-        )
-
-    swap = to_partner(struct.at[:, :, 1 - core], pair, pair_send.at[0], pair_recv.at[0])
+    swap = to_partner(struct.at[:, :, :, 1 - core], pair, pair_send.at[0], pair_recv.at[0])
     swap.start()
-    side[0, 0].start()
-    for copy in halo.values():
-        copy.start()
     for load in loads[5:]:
         load.wait()
     msg[...] = jnp.zeros_like(msg)
 
     def part_copy(k):
         return pltpu.make_async_remote_copy(
-            src_ref=chip_sum.at[:, (chip + k) % chips],
+            src_ref=chip_sum.at[:, :, (at[1] + k) % ny],
             dst_ref=parts.at[k],
             send_sem=part_send.at[k],
             recv_sem=part_recv.at[k],
-            device_id=same_core(k),
+            device_id=over_y(k),
             device_id_type=mesh_id,
         )
 
+    def line_copy(k, slot):
+        return pltpu.make_async_remote_copy(
+            src_ref=lines.at[at[0]],
+            dst_ref=lines.at[slot],
+            send_sem=line_send.at[k],
+            recv_sem=line_recv.at[k],
+            device_id=over_x(k),
+            device_id_type=mesh_id,
+        )
+
     def share_copy(k, slot):
         return pltpu.make_async_remote_copy(
-            src_ref=share,
-            dst_ref=field.at[:, slot, core],
+            src_ref=field.at[:, :, at[1], core],
+            dst_ref=field.at[:, :, slot, core],
             send_sem=share_send.at[k],
             recv_sem=share_recv.at[k],
-            device_id=same_core(k),
+            device_id=over_y(k),
             device_id_type=mesh_id,
         )
 
     def field_copy(half):
-        mine = field.at[:, :, half]
+        mine = field.at[:, :, :, half]
         return to_partner(mine, mine, pair_send.at[1], pair_recv.at[1])
 
     def sum_pair():
         swap.wait()
-        both = struct[:, :, core].astype(jnp.float32) + pair[...].astype(jnp.float32)
+        both = struct[:, :, :, core].astype(jnp.float32) + pair[...].astype(jnp.float32)
         chip_sum[...] = both.astype(jnp.bfloat16)
-
-        @pl.loop(1, chips)
-        def _(k):
+        for k in range(1, ny):
             part_copy(k).start()
 
+    def sum_parts():
+        for k in range(1, ny):
+            part_copy(k).wait()
+        parts[0] = chip_sum[:, :, at[1]]
+        lines[at[0]] = jnp.sum(parts[...].astype(jnp.float32), axis=0).astype(jnp.bfloat16)
+        for k in range(1, nx):
+            line_copy(k, at[0]).start()
+
     def filter_share():
-        @pl.loop(1, chips)
-        def _(k):
-            part_copy(k).wait()
-
-        parts[0] = chip_sum[:, chip]
-        total = jnp.sum(parts[...].astype(jnp.float32), axis=0).reshape(2 * rows, feat)
+        for k in range(1, nx):
+            line_copy(k, (at[0] - k + nx) % nx).wait()
+        total = jnp.sum(lines[...].astype(jnp.float32), axis=0).reshape(2 * nx * rows, feat)
         mixed = jnp.dot(total, mix_ref[...], precision=lax.Precision.HIGHEST, preferred_element_type=jnp.float32)
-        vec = turn_cols[pl.ds((chip * 2 + core) * rows, rows)] * (2.0 * math.pi)
+        vec = [turn_cols[pl.ds(((x * ny + at[1]) * 2 + core) * rows, rows)] for x in range(nx)]
+        vec = jnp.concatenate(vec) * (2.0 * math.pi)
         square = jnp.sum(vec * vec, axis=1, keepdims=True)
         damp = strength * jnp.exp(-0.5 * smearing * square) / (square + screening)
         damp = damp * (1.0 / math.sqrt(cells * slots * devices * waves))
         filtered = (mixed * jnp.concatenate([damp, damp])).astype(jnp.bfloat16)
         projected = jnp.dot(filtered, we_ref[...], preferred_element_type=jnp.float32)
-        projected = projected.astype(jnp.bfloat16).reshape(2, rows, feat)
-        share[...] = projected
-        field[:, chip, core] = projected
-
-        @pl.loop(1, chips)
-        def _(k):
-            share_copy(k, chip).start()
+        field[:, :, at[1], core] = projected.astype(jnp.bfloat16).reshape(2, nx, rows, feat)
+        for k in range(1, ny):
+            share_copy(k, at[1]).start()
 
     def join_field():
-        @pl.loop(1, chips)
-        def _(k):
-            share_copy(k, (chip - k + chips) % chips).wait()
-
+        for k in range(1, ny):
+            share_copy(k, (at[1] - k + ny) % ny).wait()
         field_copy(core).start()
 
     def place(x, j):
@@ -410,8 +450,17 @@
 
     def halo_in(keys):
         for key in keys:
-            halo[key].wait()
+            halo[key].wait_recv()
             side[key].start()
+
+    def face_in(step):
+        halo_in([(step, 0)])
+        halo[step, 1].start()
+        halo[step, -1].start()
+
+    def faces_in(direct):
+        for step, inside in ((1, at[0] > 0), (-1, at[0] < nx - 1)):
+            pl.when(inside if direct else jnp.logical_not(inside))(functools.partial(face_in, step))
 
     def side_in(keys):
         for key in keys:
@@ -421,20 +470,23 @@
     weigh(0, jnp.int32(0))
 
     ends = 2 * cy - 4
+    last = 3 * cy
     events = [
-        (0, sum_pair),
+        (1, sum_pair),
         (ends - 2, lambda: halo_in([(0, -1)])),
         (ends - 1, lambda: side_in([(0, -1)])),
         (ends, lambda: halo_in([(0, 1)])),
+        (ends, sum_parts),
         (ends + 1, lambda: side_in([(0, 1)])),
-        (ends + 2, lambda: halo_in([(1, 0), (-1, 0)])),
-        (ends + 2, filter_share),
+        (ends + 1, lambda: faces_in(True)),
+        (ends + 2, lambda: faces_in(False)),
         (ends + 3, lambda: side_in([(1, 0), (-1, 0)])),
-        (3 * cy - 4, lambda: halo_in([(1, -1), (-1, -1)])),
-        (3 * cy - 3, lambda: side_in([(1, -1), (-1, -1)])),
-        (3 * cy - 3, lambda: halo_in([(1, 1), (-1, 1)])),
-        (3 * cy - 2, lambda: side_in([(1, 1), (-1, 1)])),
-        (3 * cy - 1, join_field),
+        (last - 4, filter_share),
+        (last - 3, lambda: halo_in([(1, -1), (-1, -1)])),
+        (last - 3, lambda: side_in([(1, -1), (-1, -1)])),
+        (last - 2, lambda: halo_in([(1, 1), (-1, 1)])),
+        (last - 2, lambda: side_in([(1, 1), (-1, 1)])),
+        (last - 1, join_field),
     ]
 
     @pl.loop(0, 3 * cy)
@@ -446,6 +498,8 @@
         weigh(0, j + 1)
         gather(1, j)
 
+    for copy in halo.values():
+        copy.wait_send()
     field_copy(core).wait_send()
     field_copy(1 - core).wait_recv()
 
@@ -527,8 +581,9 @@
     fold_z = grid[2] == 2 and cz == 1
     counts = tuple(lax.axis_size(n) for n in axes)
     rows = waves // devices
-    chips = counts[0] * counts[1]
-    if fold_z and rows % 16 == 0 and min(counts) > 1 and cx == 2 and cy > 2 and 4 * cells <= slots == 128:
+    nx, ny = counts[:2]
+    known = 2 < nx < 5
+    if fold_z and known and rows % 16 == 0 and ny > 2 and cx == 2 and cy > 2 and 4 * cells <= slots == 128:
         vmem = pl.BlockSpec(memory_space=pltpu.VMEM)
         dma = pltpu.SemaphoreType.DMA
         out = pl.pallas_call(
@@ -556,22 +611,25 @@
                 pltpu.VMEM((2, 3, levels * slots, 2 * slots), jnp.bfloat16),
                 pltpu.VMEM((cells, slots, feat), jnp.float32),
                 pltpu.VMEM((2 * waves, cells * slots), jnp.bfloat16),
-                pltpu.VMEM((2, chips, 2, rows, feat), jnp.bfloat16),
-                pltpu.VMEM((2, chips, rows, feat), jnp.bfloat16),
-                pltpu.VMEM((2, chips, rows, feat), jnp.bfloat16),
-                pltpu.VMEM((chips, 2, rows, feat), jnp.bfloat16),
-                pltpu.VMEM((2, rows, feat), jnp.bfloat16),
-                pltpu.VMEM((2, chips, 2, rows, feat), jnp.bfloat16),
+                pltpu.VMEM((2, nx, ny, 2, rows, feat), jnp.bfloat16),
+                pltpu.VMEM((2, nx, ny, rows, feat), jnp.bfloat16),
+                pltpu.VMEM((2, nx, ny, rows, feat), jnp.bfloat16),
+                pltpu.VMEM((ny, 2, nx, rows, feat), jnp.bfloat16),
+                pltpu.VMEM((nx, 2, nx, rows, feat), jnp.bfloat16),
+                pltpu.VMEM((2, nx, ny, 2, rows, feat), jnp.bfloat16),
+                pltpu.SemaphoreType.REGULAR((2,)),
                 dma((8,)),
                 dma((8,)),
                 dma((9,)),
                 dma((9,)),
                 dma((2,)),
                 dma((2,)),
-                dma((chips,)),
-                dma((chips,)),
-                dma((chips,)),
-                dma((chips,)),
+                dma((ny,)),
+                dma((ny,)),
+                dma((nx,)),
+                dma((nx,)),
+                dma((ny,)),
+                dma((ny,)),
             ],
             compiler_params=pltpu.CompilerParams(
                 collective_id=0, has_side_effects=True, vmem_limit_bytes=56 * 2**20

time: 48.7 us -> 37.7 us (0.77)
  Pallas kernels: 47.8 us -> 36.7 us
    pallas_call x1, Pallas kernels: 47.8 us -> 36.7 us  [body(): pl.pallas_call(functools.partial(layer_kernel, counts, levels), in_specs=...]
where the time goes in v3:
time: 37.7 us; the launch traced here: 37.5 us
  Pallas kernels  36.7 us (97%)
  local copies, waits for them, and re-layouts  0.8 us (2%)
    pallas_call x1, Pallas kernels, body(): pl.pallas_call(functools.partial(layer_kernel, counts, levels), in_specs=...  36.7 us
    unnamed x1, local copies, waits for them, and re-layouts  0.8 us

profile of v3, /device:TPU:0, one launch (start us, length us, event | category | flops | bytes accessed | tf_op | source)
XLA Modules:
  0.0 37.5 jit_solution(17544542048239874543)
XLA Ops:
  0.0 36.7 %layer.1 = bf16[8,128,256]{2,1,0:T(8,128)(2,1)S(1)} custom-call(bf16[2,4,128,256]{3,2,1,0:T(8,128)(2,1)} %bitcast.12, bf16[2,3,4,128]{3,2,1,0:T(4,128)(2,1)} %bitcast.13, s32[8,128]{1,0:T(8,128)} %bitcast.14, s32[3,512]{1,0:T(4,128)} %index_in.1, f32[4,8]{1,0:T(4,128)} %bitcast.15, f32[256,256]{1,0:T(8,128)} %mix_in.1, bf16[256,256]{1,0:T(8,128)(2,1)} %we_in.1, ...), custom_call_target="tpu_custom_call" | custom-call | tf_op jit(solution)/shard_map/layer/pallas_call | solution.py:589
  36.7 0.8 %copy.13 = bf16[2,4,1,128,256]{4,3,2,1,0:T(8,128)(2,1)} copy(bf16[2,4,1,128,256]{4,3,2,1,0:T(8,128)(2,1)S(1)} %bitcast.11) | data formatting | bytes 1048576

commit v4 on v3

--- a/solution.py
+++ b/solution.py
@@ -15,6 +15,9 @@
 
 SIN_C = [(-1.0) ** k * math.pi ** (2 * k + 1) / math.factorial(2 * k + 1) for k in range(7)]
 COS_C = [(-1.0) ** k * math.pi ** (2 * k) / math.factorial(2 * k) for k in range(7)]
+
+SIN_P = [3.1415926401839953, -5.167710090331888, 2.550077659731212, -0.5982921594834444, 0.07765940825518475]
+COS_P = [0.9999999534666585, -4.934792858674198, 4.058411914145813, -1.3318801611126891, 0.21969679833109643]
 
 
 def poly(z, coefs):
@@ -145,6 +148,7 @@
     in_sem,
     wide,
     rows_sc,
+    pos_sc,
     out_mask,
     turn_cols,
     wb,
@@ -152,6 +156,8 @@
     phi,
     msg,
     basis,
+    basis_t,
+    joined,
     struct,
     pair,
     chip_sum,
@@ -186,8 +192,8 @@
     pad = wide.shape[3] - slots
     reach = 2.0 * sharpness / (levels - 1) * math.log2(math.e)
     partner = (at[0], at[1], 1 - core)
-    lower = (at[0] + nx - 1) // nx
-    upper = (2 * nx - 2 - at[0]) // nx
+    line_near = (at[0] + nx - 1) // nx + (2 * nx - 2 - at[0]) // nx
+    bits = [1 << n for n in range(ny.bit_length() - 1)]
 
     def over_x(k):
         return ((at[0] + k + nx) % nx, at[1], core)
@@ -217,13 +223,17 @@
         def _():
             pl.semaphore_signal(sem, inc=1, device_id=over_x(1), device_id_type=mesh_id)
 
+    def greet_near(sem):
+        greet_line(sem)
+        for bit in bits:
+            step = bit * (1 - 2 * (at[1] // bit % 2))
+            pl.semaphore_signal(sem, inc=1, device_id=over_y(step), device_id_type=mesh_id)
+
     pl.semaphore_signal(barrier, inc=1, device_id=partner, device_id_type=mesh_id)
-    greet_line(barrier)
-    for k in range(1, ny):
-        pl.semaphore_signal(barrier, inc=1, device_id=over_y(k), device_id_type=mesh_id)
-
-    for load in loads[:4]:
-        load.wait()
+    greet_near(barrier)
+
+    loads[0].wait()
+    loads[1].wait()
     rows_sc[...] = jnp.zeros_like(rows_sc)
     for x in range(cx):
         for a in range(3):
@@ -273,31 +283,70 @@
         for step, inside in ((1, at[0] < nx - 1), (-1, at[0] > 0)):
             pl.when(inside if direct else jnp.logical_not(inside))(halo[step, 0].start)
 
-    def open_links():
-        pl.semaphore_wait(barrier, 1 + lower + upper + ny - 1)
-        greet_line(token.at[0])
-        side[0, 0].start()
-        halo[0, 1].start()
-        halo[0, -1].start()
-        send_faces(True)
+    def send_rows(direct):
+        for step, near in ((1, at[1] % 2 == 0), (-1, at[1] % 2 == 1)):
+            pl.when(near if direct else jnp.logical_not(near))(halo[0, step].start)
 
     def pass_token():
-        pl.semaphore_wait(token.at[0], lower + upper)
+        pl.semaphore_wait(token.at[0], line_near + len(bits))
         greet_line(token.at[1])
+        send_rows(False)
 
     def open_wrap():
-        pl.semaphore_wait(token.at[1], lower + upper)
+        pl.semaphore_wait(token.at[1], line_near)
         send_faces(False)
 
+    pl.semaphore_wait(barrier, 1 + line_near + len(bits))
+    greet_near(token.at[0])
+    send_rows(True)
+    send_faces(True)
+    side[0, 0].start()
+
+    loads[2].wait()
+    for w0 in range(0, waves, 128):
+        part = [index_ref[a : a + 1, w0 : w0 + 128].astype(jnp.float32) * (1.0 / grid[a]) for a in range(3)]
+        part = jnp.concatenate(part + [jnp.zeros((5, 128), jnp.float32)])
+        turn_cols[w0 : w0 + 128] = part.T
+    for x in range(cx):
+        for y in range(cy):
+            start = [at[0] * cx + x, at[1] * cy + y, core]
+            cell = x * cy + y
+            for a in range(3):
+                k = (x * 3 + a) * cy + y
+                pos_sc[a : a + 1, cell * slots : (cell + 1) * slots] = rows_sc[k : k + 1] + start[a].astype(jnp.float32)
+
+    @pl.loop(0, cells // 2)
+    def _(two):
+        pl.when(two == cells // 8)(pass_token)
+        pl.when(two == cells // 4 + 1)(open_wrap)
+        lanes = pl.ds(pl.multiple_of(two * 2 * slots, 2 * slots), 2 * slots)
+        pos = pos_sc[:, lanes]
+        chunk = 32
+        for w0 in range(0, waves, chunk):
+            wv = turn_cols[w0 : w0 + chunk]
+            turns = wv[:, 0:1] * pos[0:1] + wv[:, 1:2] * pos[1:2] + wv[:, 2:3] * pos[2:3]
+            u = turns - jnp.round(turns)
+            q = u * u
+            s = u * poly(q, [v * math.sqrt(2.0) for v in SIN_P])
+            c = poly(q, [v * math.sqrt(2.0) for v in COS_P])
+            basis[w0 : w0 + chunk, lanes] = (1.0 - s * s).astype(jnp.bfloat16)
+            basis[waves + w0 : waves + w0 + chunk, lanes] = (s * c).astype(jnp.bfloat16)
+
+    atoms = wide[1 : 1 + cx, 1 : 1 + cy, 0, 0:slots].reshape(cells * slots, feat)
+    struct[...] = (
+        jnp.dot(basis[...], atoms, preferred_element_type=jnp.float32)
+        .astype(jnp.bfloat16)
+        .reshape(struct.shape)
+    )
+    swap = to_partner(struct.at[:, 1 - core], pair, pair_send.at[0], pair_recv.at[0])
+    swap.start()
+
+    loads[3].wait()
     for x in range(cx):
         for y in range(cy):
             for a in range(3):
                 k = (x * 3 + a) * cy + y
                 hb[x * cy + y, a] = jnp.broadcast_to(turned[:, k : k + 1] * reach, (slots, slots))
-    for w0 in range(0, waves, 128):
-        part = [index_ref[a : a + 1, w0 : w0 + 128].astype(jnp.float32) * (1.0 / grid[a]) for a in range(3)]
-        part = jnp.concatenate(part + [jnp.zeros((5, 128), jnp.float32)])
-        turn_cols[w0 : w0 + 128] = part.T
     owner = lax.broadcasted_iota(jnp.int32, (heads, feat), 1) // (feat // heads)
     mine = owner == lax.broadcasted_iota(jnp.int32, (heads, feat), 0)
     for b in range(levels):
@@ -306,36 +355,6 @@
         column = jnp.broadcast_to(radial_ref[:, b : b + 1], (heads, feat)) * scale
         wb[b : b + 1] = jnp.sum(jnp.where(mine, column, 0.0), axis=0, keepdims=True)
 
-    @pl.loop(0, cells)
-    def _(cell):
-        x = cell // cy
-        y = cell % cy
-        first = (x * 3) * cy + y
-        start = [(at[0] * cx + x).astype(jnp.float32), (at[1] * cy + y).astype(jnp.float32), core.astype(jnp.float32)]
-        pos = [rows_sc[pl.ds(first + a * cy, 1)] + start[a] for a in range(3)]
-        lanes = pl.ds(pl.multiple_of(cell * slots, slots), slots)
-        pl.when(cell == 0)(open_links)
-        pl.when(cell == cells // 4)(pass_token)
-        pl.when(cell == cells // 2 + 1)(open_wrap)
-        chunk = 64
-        for w0 in range(0, waves, chunk):
-            wv = turn_cols[w0 : w0 + chunk]
-            turns = wv[:, 0:1] * pos[0] + wv[:, 1:2] * pos[1] + wv[:, 2:3] * pos[2]
-            u = turns - jnp.floor(turns + 0.5)
-            q = u * u
-            s = u * poly(q, SIN_C)
-            c = poly(q, COS_C)
-            basis[w0 : w0 + chunk, lanes] = (1.0 - 2.0 * s * s).astype(jnp.bfloat16)
-            basis[waves + w0 : waves + w0 + chunk, lanes] = (2.0 * s * c).astype(jnp.bfloat16)
-
-    atoms = wide[1 : 1 + cx, 1 : 1 + cy, 0, 0:slots].reshape(cells * slots, feat)
-    struct[...] = (
-        jnp.dot(basis[...], atoms, preferred_element_type=jnp.float32)
-        .astype(jnp.bfloat16)
-        .reshape(struct.shape)
-    )
-    swap = to_partner(struct.at[:, :, :, 1 - core], pair, pair_send.at[0], pair_recv.at[0])
-    swap.start()
     for load in loads[5:]:
         load.wait()
     msg[...] = jnp.zeros_like(msg)
@@ -362,8 +381,8 @@
 
     def share_copy(k, slot):
         return pltpu.make_async_remote_copy(
-            src_ref=field.at[:, :, at[1], core],
-            dst_ref=field.at[:, :, slot, core],
+            src_ref=field.at[:, core, :, at[1]],
+            dst_ref=field.at[:, core, :, slot],
             send_sem=share_send.at[k],
             recv_sem=share_recv.at[k],
             device_id=over_y(k),
@@ -371,12 +390,12 @@
         )
 
     def field_copy(half):
-        mine = field.at[:, :, :, half]
+        mine = field.at[:, half]
         return to_partner(mine, mine, pair_send.at[1], pair_recv.at[1])
 
     def sum_pair():
         swap.wait()
-        both = struct[:, :, :, core].astype(jnp.float32) + pair[...].astype(jnp.float32)
+        both = struct[:, core].astype(jnp.float32) + pair[...].astype(jnp.float32)
         chip_sum[...] = both.astype(jnp.bfloat16)
         for k in range(1, ny):
             part_copy(k).start()
@@ -394,14 +413,14 @@
             line_copy(k, (at[0] - k + nx) % nx).wait()
         total = jnp.sum(lines[...].astype(jnp.float32), axis=0).reshape(2 * nx * rows, feat)
         mixed = jnp.dot(total, mix_ref[...], precision=lax.Precision.HIGHEST, preferred_element_type=jnp.float32)
-        vec = [turn_cols[pl.ds(((x * ny + at[1]) * 2 + core) * rows, rows)] for x in range(nx)]
+        vec = [turn_cols[pl.ds(((core * nx + x) * ny + at[1]) * rows, rows)] for x in range(nx)]
         vec = jnp.concatenate(vec) * (2.0 * math.pi)
         square = jnp.sum(vec * vec, axis=1, keepdims=True)
         damp = strength * jnp.exp(-0.5 * smearing * square) / (square + screening)
         damp = damp * (1.0 / math.sqrt(cells * slots * devices * waves))
         filtered = (mixed * jnp.concatenate([damp, damp])).astype(jnp.bfloat16)
         projected = jnp.dot(filtered, we_ref[...], preferred_element_type=jnp.float32)
-        field[:, :, at[1], core] = projected.astype(jnp.bfloat16).reshape(2, nx, rows, feat)
+        field[:, core, :, at[1]] = projected.astype(jnp.bfloat16).reshape(2, nx, rows, feat)
         for k in range(1, ny):
             share_copy(k, at[1]).start()
 
@@ -486,13 +505,14 @@
         (last - 3, lambda: side_in([(1, -1), (-1, -1)])),
         (last - 2, lambda: halo_in([(1, 1), (-1, 1)])),
         (last - 2, lambda: side_in([(1, 1), (-1, 1)])),
-        (last - 1, join_field),
     ]
 
     @pl.loop(0, 3 * cy)
     def _(j):
         for when, what in events:
             pl.when(j == when)(what)
+        cell = j % cells
+        basis_t[cell] = basis[:, pl.ds(pl.multiple_of(cell * slots, slots), slots)].T
         weigh(1, j)
         gather(0, j)
         weigh(0, j + 1)
@@ -500,24 +520,39 @@
 
     for copy in halo.values():
         copy.wait_send()
+
+    half = waves // 2
+    two = 2 * slots
+
+    def far_of(pair_of_cells, half_of):
+        c0 = pair_of_cells * 2
+        first = pl.multiple_of(half_of * half, half)
+        left = jnp.concatenate([basis_t[pl.ds(c0, 2), :, pl.ds(k * waves + first, half)] for k in range(2)], axis=2)
+        right = field[:, half_of].reshape(waves, feat)
+        return jnp.dot(left.reshape(two, waves), right, preferred_element_type=jnp.float32)
+
+    @pl.loop(0, cells // 2)
+    def _(n):
+        near = msg[pl.ds(2 * n, 2)].reshape(two, feat).astype(jnp.bfloat16)
+        joined[n] = jnp.dot(near, wm_ref[...], preferred_element_type=jnp.float32)
+
+    join_field()
+
+    @pl.loop(0, cells // 2)
+    def _(n):
+        joined[n] += far_of(n, core)
+
     field_copy(core).wait_send()
     field_copy(1 - core).wait_recv()
 
-    waves_field = field[...].reshape(2 * waves, feat)
-
-    @pl.loop(0, cells)
-    def _(cell):
-        lanes = pl.ds(pl.multiple_of(cell * slots, slots), slots)
-        far = lax.dot_general(
-            basis[:, lanes], waves_field, (((0,), (0,)), ((), ())), preferred_element_type=jnp.float32
-        )
-        near = msg[cell].astype(jnp.bfloat16)
-        joined = far + jnp.dot(near, wm_ref[...], preferred_element_type=jnp.float32)
-        hidden = (joined / (1.0 + jnp.exp(-joined))).astype(jnp.bfloat16)
-        atom = wide[1 + cell // cy, 1 + cell % cy, 0, 0:slots].astype(jnp.float32)
-        result = jnp.dot(hidden, wo_ref[...], preferred_element_type=jnp.float32)
-        there = out_mask[cell]
-        out_ref[cell] = (atom + result * there).astype(jnp.bfloat16)
+    @pl.loop(0, cells // 2)
+    def _(n):
+        total = joined[n] + far_of(n, 1 - core)
+        hidden = (total / (1.0 + jnp.exp(-total))).astype(jnp.bfloat16)
+        result = jnp.dot(hidden, wo_ref[...], preferred_element_type=jnp.float32).reshape(2, slots, feat)
+        c0 = 2 * n
+        atom = wide[1 + c0 // cy, pl.ds(1 + c0 % cy, 2), 0, 0:slots].astype(jnp.float32)
+        out_ref[pl.ds(c0, 2)] = (atom + result * out_mask[pl.ds(c0, 2)]).astype(jnp.bfloat16)
 
 
 def radial_chain(gx, gy, gz, levels, reach, diagonal, p0, phi, slots):
@@ -582,7 +617,7 @@
     counts = tuple(lax.axis_size(n) for n in axes)
     rows = waves // devices
     nx, ny = counts[:2]
-    known = 2 < nx < 5
+    known = 2 < nx < 5 and ny == 4 and waves % 512 == 0 and cy % 2 == 0
     if fold_z and known and rows % 16 == 0 and ny > 2 and cx == 2 and cy > 2 and 4 * cells <= slots == 128:
         vmem = pl.BlockSpec(memory_space=pltpu.VMEM)
         dma = pltpu.SemaphoreType.DMA
@@ -604,6 +639,7 @@
                 dma((9,)),
                 pltpu.VMEM((cx + 2, cy + 2, 2, slots + 8, feat), jnp.bfloat16),
                 pltpu.VMEM((slots, slots), jnp.float32),
+                pltpu.VMEM((3, cells * slots), jnp.float32),
                 pltpu.VMEM((cells, slots, feat), jnp.float32),
                 pltpu.VMEM((waves, 8), jnp.float32),
                 pltpu.VMEM((levels, feat), jnp.float32),
@@ -611,12 +647,14 @@
                 pltpu.VMEM((2, 3, levels * slots, 2 * slots), jnp.bfloat16),
                 pltpu.VMEM((cells, slots, feat), jnp.float32),
                 pltpu.VMEM((2 * waves, cells * slots), jnp.bfloat16),
-                pltpu.VMEM((2, nx, ny, 2, rows, feat), jnp.bfloat16),
+                pltpu.VMEM((cells, slots, 2 * waves), jnp.bfloat16),
+                pltpu.VMEM((cells // 2, 2 * slots, feat), jnp.float32),
+                pltpu.VMEM((2, 2, nx, ny, rows, feat), jnp.bfloat16),
                 pltpu.VMEM((2, nx, ny, rows, feat), jnp.bfloat16),
                 pltpu.VMEM((2, nx, ny, rows, feat), jnp.bfloat16),
                 pltpu.VMEM((ny, 2, nx, rows, feat), jnp.bfloat16),
                 pltpu.VMEM((nx, 2, nx, rows, feat), jnp.bfloat16),
-                pltpu.VMEM((2, nx, ny, 2, rows, feat), jnp.bfloat16),
+                pltpu.VMEM((2, 2, nx, ny, rows, feat), jnp.bfloat16),
                 pltpu.SemaphoreType.REGULAR((2,)),
                 dma((8,)),
                 dma((8,)),

time: 37.7 us -> 36.9 us (0.979)
  Pallas kernels: 36.7 us -> 35.9 us
    pallas_call x1, Pallas kernels: 36.7 us -> 35.9 us  [body(): pl.pallas_call(functools.partial(layer_kernel, counts, levels), in_specs=...]
where the time goes in v4:
time: 36.9 us; the launch traced here: 36.7 us
  Pallas kernels  35.9 us (97%)
  local copies, waits for them, and re-layouts  0.8 us (2%)
    pallas_call x1, Pallas kernels, body(): pl.pallas_call(functools.partial(layer_kernel, counts, levels), in_specs=...  35.9 us
    unnamed x1, local copies, waits for them, and re-layouts  0.8 us

profile of v4, /device:TPU:0, one launch (start us, length us, event | category | flops | bytes accessed | tf_op | source)
XLA Modules:
  0.0 36.7 jit_solution(16197754493793395176)
XLA Ops:
  0.0 35.9 %layer.1 = bf16[8,128,256]{2,1,0:T(8,128)(2,1)S(1)} custom-call(bf16[2,4,128,256]{3,2,1,0:T(8,128)(2,1)} %bitcast.12, bf16[2,3,4,128]{3,2,1,0:T(4,128)(2,1)} %bitcast.13, s32[8,128]{1,0:T(8,128)} %bitcast.14, s32[3,512]{1,0:T(4,128)} %index_in.1, f32[4,8]{1,0:T(4,128)} %bitcast.15, f32[256,256]{1,0:T(8,128)} %mix_in.1, bf16[256,256]{1,0:T(8,128)(2,1)} %we_in.1, ...), custom_call_target="tpu_custom_call" | custom-call | tf_op jit(solution)/shard_map/layer/pallas_call | solution.py:624
  35.9 0.8 %copy.13 = bf16[2,4,1,128,256]{4,3,2,1,0:T(8,128)(2,1)} copy(bf16[2,4,1,128,256]{4,3,2,1,0:T(8,128)(2,1)S(1)} %bitcast.11) | data formatting | bytes 1048576
